TPU v7x, 512 devices: a whole 4x8x8 slice. The times are simulated.
512 devices in a mesh: win: 64 (over z_hi, y, core), head: 8 (over x, z_lo).
Axes of the slice: x: 4, y: 8, z: 8 (z_hi: 4, z_lo: 2; z = z_hi * 2 + z_lo), core: 2. Of those that a mesh axis runs over, the one named last changes fastest.
Arguments:
- qkv: bfloat16 [3, 64, 96, 48, 1024], P(None, 'win', 'head'), may hold values from -10 to 10
Outputs:
- attended: bfloat16 [64, 96, 48, 1024], P('win', 'head')
All inputs are finite; a program needn't handle non-finite values.
Results may differ from a plain program's by a relative error of at most 0.0047.
Values may be sent and summed in bfloat16 or wider, within the bound.
No kernel may reach another device: no remote copies, remote signals or barrier semaphores. Data moves between devices by JAX's collectives and lax.ppermute only.
A program may use at most 64 MiB of HBM per device.

v0:
```python
import math

import jax
import jax.numpy as jnp
from jax import lax
from jax.sharding import PartitionSpec as P

HEAD_DIM = 128


def from_behind(shard, axis, by):
    count = lax.axis_size(axis)
    return lax.ppermute(shard, axis, [(i, (i + by) % count) for i in range(count)])


def in_blocks(shard, dim, count):
    shape = shard.shape
    tiles = shard.reshape(*shape[:dim], count, shape[dim] // count, *shape[dim + 1 :])
    return jnp.moveaxis(tiles, dim, 0)


def cut_rows(length, count):
    hop = length // count
    if hop >= 8:
        hop -= hop % 8
    return [hop * k for k in range(1, count)]


def laid_out(tiles, dim):
    shape = list(tiles.shape[1:])
    shape[dim] *= tiles.shape[0]
    return jnp.moveaxis(tiles, 0, dim).reshape(shape)


def several_exchanges(shard, axis, pieces, split_dim, concat_dim):
    tiles = in_blocks(shard, split_dim, lax.axis_size(axis))
    widest = max(range(1, max(2, tiles.ndim - 1)), key=lambda d: tiles.shape[d])
    outs = []
    for share in jnp.split(tiles, cut_rows(tiles.shape[widest], pieces), axis=widest):
        if share.size:
            outs.append(lax.all_to_all(share, axis, split_axis=0, concat_axis=0, tiled=True))
    return laid_out(jnp.concatenate(outs, axis=widest), concat_dim)


def partner(value, axis, apart):
    mask = 2**apart
    pairs = [(source, source ^ mask) for source in range(lax.axis_size(axis))]
    return lax.ppermute(value, axis, pairs)


def attend(queries, keys, values, labels_query, labels_key):
    query_count, head_count, head_width = queries.shape
    block_rows = math.gcd(query_count, 576)
    score_scale = 1.0 / math.sqrt(head_width)

    def one_block(pieces):
        query_block, label_block = pieces
        scores = (
            jnp.einsum("qhd,khd->hqk", query_block, keys, preferred_element_type=jnp.float32)
            * score_scale
        )
        allowed = label_block[:, None] == labels_key[None, :]
        scores = jnp.where(allowed[None], scores, -jnp.inf)
        row_max = jnp.max(scores, axis=-1, keepdims=True)
        weights = jnp.exp(scores - row_max)
        row_total = jnp.sum(weights, axis=-1, keepdims=True)
        mixture = jnp.einsum(
            "hqk,khd->qhd", weights.astype(jnp.bfloat16), values, preferred_element_type=jnp.float32
        )
        return (mixture / jnp.transpose(row_total, (1, 0, 2))).astype(jnp.bfloat16)

    query_blocks = queries.reshape(query_count // block_rows, block_rows, head_count, head_width)
    label_blocks = labels_query.reshape(query_count // block_rows, block_rows)
    return lax.map(one_block, (query_blocks, label_blocks)).reshape(
        query_count, head_count, head_width
    )


def window_attention(window, labels):
    row_count, side_cells, channels = (window.shape[1], window.shape[2], window.shape[3])
    head_count = channels // HEAD_DIM
    window_parts = window.reshape(
        3, row_count // side_cells, side_cells * side_cells, head_count, HEAD_DIM
    )
    label_parts = labels.reshape(row_count // side_cells, side_cells * side_cells)
    outputs = []
    for window_row in range(row_count // side_cells):
        outputs.append(
            attend(
                window_parts[0, window_row],
                window_parts[1, window_row],
                window_parts[2, window_row],
                label_parts[window_row],
                label_parts[window_row],
            )
        )
    return jnp.stack(outputs).reshape(row_count, side_cells, channels)


def body(qkv):
    side_cells = qkv.shape[3]
    half_cols = side_cells // 2
    tokens = qkv[:, 0]
    arrived = from_behind(tokens[:, :, :half_cols], "win", -2)
    tokens = jnp.concatenate([tokens[:, :, half_cols:], arrived], axis=2)
    head_view = several_exchanges(tokens, "head", 2, 3, 1)
    half_rows = head_view.shape[1]
    crossing = partner(head_view[:, :half_cols], "win", 0)
    extended = jnp.concatenate([head_view[:, half_cols:], crossing], axis=1)
    lat_half = lax.axis_index("win") % 2
    row_index = jnp.arange(half_rows, dtype=jnp.int32)[:, None]
    wrapped = jnp.logical_and(lat_half == 1, row_index >= half_rows - half_cols)
    labels = jnp.broadcast_to(jnp.where(wrapped, 1, 0).astype(jnp.int32), (half_rows, side_cells))
    result = window_attention(extended, labels)
    returned = partner(result[half_rows - half_cols :], "win", 0)
    row_fixed = jnp.concatenate([returned, result[: half_rows - half_cols]], axis=0)
    restored = lax.all_to_all(row_fixed, "head", split_axis=0, concat_axis=2, tiled=True)
    from_west = from_behind(restored[:, half_cols:], "win", 2)
    restored = jnp.concatenate([from_west, restored[:, :half_cols]], axis=1)
    return restored[None]


def solution(mesh):
    in_specs = (P(None, "win", "head", None, None),)
    out_specs = P("win", "head", None, None)
    return jax.shard_map(body, mesh=mesh, in_specs=in_specs, out_specs=out_specs, check_vma=False)
```

profile of v0, /device:TPU:1, one launch (start us, length us, event | category | flops | bytes accessed | tf_op | source)
XLA Modules:
  0.0 251.8 jit_solution(8048026713764120286)
XLA Ops:
  0.0 2.4 fusion.57
  2.4 14.4 %collective-permute-start = (bf16[3,12,24,1024]{3,2,1,0:T(8,128)(2,1)S(1)}, bf16[3,12,24,1024]{3,2,1,0:T(8,128)(2,1)S(1)}, u32[]{:S(2)}, u32[]{:S(2)}) collective-permute-start(bf16[3,12,24,1024]{3,2,1,0:T(8,128)(2,1)S(1)} %get-tuple-element.213), channel_id=1, source_target_pairs={{0,496},{8,504},{16,0},{24,8},{32,16},{40,24},{48,32},{56,40},{64,... | collective-permute-start | bytes 5308424 | tf_op jit(solution)/shard_map/ppermute | solution.py:13
  16.8 69.5 %collective-permute-done = bf16[3,12,24,1024]{3,2,1,0:T(8,128)(2,1)S(1)} collective-permute-done((bf16[3,12,24,1024]{3,2,1,0:T(8,128)(2,1)S(1)}, bf16[3,12,24,1024]{3,2,1,0:T(8,128)(2,1)S(1)}, u32[]{:S(2)}, u32[]{:S(2)}) %collective-permute-start) | collective-permute-done | bytes 1769504 | tf_op jit(solution)/shard_map/ppermute | solution.py:13
  86.8 0.9 copy.37
  88.0 1.5 copy.22
  89.5 7.7 %all-to-all-start = ((bf16[8,3,12,24,128]{4,3,2,1,0:T(8,128)(2,1)}), bf16[8,3,12,24,128]{4,3,2,1,0:T(8,128)(2,1)S(1)}, u32[]{:S(2)}, u32[]{:S(2)}) async-start(bf16[8,3,12,24,128]{4,3,2,1,0:T(8,128)(2,1)} %copy.22), calls=%async_computation | async-start | bytes 3538944 | tf_op jit(solution)/shard_map/all_to_all | solution.py:41
  97.2 1.5 copy.23
  98.7 19.1 %all-to-all-done = bf16[8,3,12,24,128]{4,3,2,1,0:T(8,128)(2,1)S(1)} async-done(((bf16[8,3,12,24,128]{4,3,2,1,0:T(8,128)(2,1)}), bf16[8,3,12,24,128]{4,3,2,1,0:T(8,128)(2,1)S(1)}, u32[]{:S(2)}, u32[]{:S(2)}) %all-to-all-start) | async-done | bytes 1769504 | tf_op jit(solution)/shard_map/all_to_all | solution.py:41
  117.7 25.5 %all_to_all.28 = bf16[8,3,12,24,128]{4,3,2,1,0:T(8,128)(2,1)S(1)} all-to-all(bf16[8,3,12,24,128]{4,3,2,1,0:T(8,128)(2,1)} %copy.23), channel_id=1, replica_groups=mesh['win'=64,'head'=8] {'head'}, dimensions={0} | all-to-all | bytes 3538944 | tf_op jit(solution)/shard_map/all_to_all | solution.py:41
  143.3 1.0 pad_maximum_fusion.1
  144.9 1.0 slice.95
  145.8 5.5 %collective-permute-start.1 = (bf16[3,24,48,128]{3,2,1,0:T(8,128)(2,1)}, bf16[3,24,48,128]{3,2,1,0:T(8,128)(2,1)}, u32[]{:S(2)}, u32[]{:S(2)}) collective-permute-start(bf16[3,24,48,128]{3,2,1,0:T(8,128)(2,1)} %slice.95), channel_id=1, source_target_pairs={{0,8},{8,0},{16,24},{24,16},{32,40},{40,32},{48,56},{56,48},{64,72... | collective-permute-start | bytes 2654216 | tf_op jit(solution)/shard_map/ppermute | solution.py:48
  152.7 1.4 broadcast_in_dim.57
  156.2 1.5 pad_maximum_fusion.2
  157.7 1.0 slice_bitcast_fusion.2
  158.7 0.8 slice.96
  159.6 19.8 %while.22 = (s32[]{:T(128)}, bf16[4,576,1,128]{3,1,2,0:T(8,128)(2,1)S(1)}, s32[4,576]{1,0:T(4,128)}, bf16[4,576,1,128]{3,1,2,0:T(8,128)(2,1)}, bf16[2304,1,128]{...) while((s32[]{:T(128)}, ...), condition=%wide.region_3.4_spmd.clone, body=%wide.region_0.3_spmd.clone.sunk | while | flops 690240384 | bytes 17459484 | solution.py:74
  160.5 2.2 fusion.71
  162.7 0.9 fusion.72
  163.6 1.0 fusion.73
  165.5 2.2 fusion.71
  167.7 0.9 fusion.72
  168.6 1.0 fusion.73
  170.4 2.2 fusion.71
  172.7 0.9 fusion.72
  173.5 1.0 fusion.73
  175.4 2.2 fusion.71
  177.6 0.9 fusion.72
  178.5 1.0 fusion.73
  179.6 12.5 %while.23 = (s32[]{:T(128)}, bf16[4,576,1,128]{3,1,2,0:T(8,128)(2,1)S(1)}, s32[4,576]{1,0:T(4,128)S(1)}, bf16[4,576,1,128]{3,1,2,0:T(8,128)(2,1)S(1)}, bf16[2304...) while((s32[]{:T(128)}, ...), condition=%wide.region_7.8_spmd.clone, body=%wide.region_4.7_spmd.clone.sunk | while | flops 690240384 | bytes 17463840 | solution.py:74
  179.8 1.1 fusion.76
  180.8 0.9 fusion.77
  181.7 1.0 fusion.78
  182.9 1.1 fusion.76
  184.0 0.9 fusion.77
  184.8 1.0 fusion.78
  186.0 1.1 fusion.76
  187.1 0.9 fusion.77
  188.0 1.0 fusion.78
  189.1 1.1 fusion.76
  190.2 0.9 fusion.77
  191.1 1.0 fusion.78
  192.2 1.9 collective-permute-start.2
  194.2 1.5 collective-permute-done.2
  195.8 19.3 %all_to_all.29 = bf16[96,48,128]{2,1,0:T(8,128)(2,1)S(1)} all-to-all(bf16[96,48,128]{2,1,0:T(8,128)(2,1)S(1)} %pad_maximum_fusion.4), channel_id=1, replica_groups=mesh['win'=64,'head'=8] {'head'}, dimensions={0} | all-to-all | bytes 2359296 | tf_op jit(solution)/shard_map/all_to_all | solution.py:117
  215.6 1.9 collective-permute-start.3
  217.5 33.1 %collective-permute-done.3 = bf16[12,24,1024]{2,1,0:T(8,128)(2,1)S(1)} collective-permute-done((bf16[12,24,1024]{2,1,0:T(8,128)(2,1)S(1)}, bf16[12,24,1024]{2,1,0:T(8,128)(2,1)S(1)}, u32[]{:S(2)}, u32[]{:S(2)}) %collective-permute-start.3) | collective-permute-done | bytes 589856 | tf_op jit(solution)/shard_map/ppermute | solution.py:13
  250.6 1.1 maximum_bitcast_fusion
  (46 shorter events, 9.8 us)
Async XLA Ops:
  2.4 83.9 %collective-permute-start = (bf16[3,12,24,1024]{3,2,1,0:T(8,128)(2,1)S(1)}, bf16[3,12,24,1024]{3,2,1,0:T(8,128)(2,1)S(1)}, u32[]{:S(2)}, u32[]{:S(2)}) collective-permute-start(bf16[3,12,24,1024]{3,2,1,0:T(8,128)(2,1)S(1)} %get-tuple-element.213), channel_id=1, source_target_pairs={{0,496},{8,504},{16,0},{24,8},{32,16},{40,24},{48,32},{56,40},{64,... | collective-permute-start | bytes 5308424 | tf_op jit(solution)/shard_map/ppermute | solution.py:13
  89.5 28.3 %all-to-all-start = ((bf16[8,3,12,24,128]{4,3,2,1,0:T(8,128)(2,1)}), bf16[8,3,12,24,128]{4,3,2,1,0:T(8,128)(2,1)S(1)}, u32[]{:S(2)}, u32[]{:S(2)}) async-start(bf16[8,3,12,24,128]{4,3,2,1,0:T(8,128)(2,1)} %copy.22), calls=%async_computation | async-start | bytes 3538944 | tf_op jit(solution)/shard_map/all_to_all | solution.py:41
  145.8 10.3 %collective-permute-start.1 = (bf16[3,24,48,128]{3,2,1,0:T(8,128)(2,1)}, bf16[3,24,48,128]{3,2,1,0:T(8,128)(2,1)}, u32[]{:S(2)}, u32[]{:S(2)}) collective-permute-start(bf16[3,24,48,128]{3,2,1,0:T(8,128)(2,1)} %slice.95), channel_id=1, source_target_pairs={{0,8},{8,0},{16,24},{24,16},{32,40},{40,32},{48,56},{56,48},{64,72... | collective-permute-start | bytes 2654216 | tf_op jit(solution)/shard_map/ppermute | solution.py:48
  157.7 2.0 copy-start
  192.2 3.5 %collective-permute-start.2 = (bf16[24,48,128]{2,1,0:T(8,128)(2,1)S(1)}, bf16[24,48,128]{2,1,0:T(8,128)(2,1)S(1)}, u32[]{:S(2)}, u32[]{:S(2)}) collective-permute-start(bf16[24,48,128]{2,1,0:T(8,128)(2,1)S(1)} %slice.102), channel_id=1, source_target_pairs={{0,8},{8,0},{16,24},{24,16},{32,40},{40,32},{48,56},{56,48},{64,72... | collective-permute-start | bytes 884744 | tf_op jit(solution)/shard_map/ppermute | solution.py:48
  215.6 35.1 %collective-permute-start.3 = (bf16[12,24,1024]{2,1,0:T(8,128)(2,1)S(1)}, bf16[12,24,1024]{2,1,0:T(8,128)(2,1)S(1)}, u32[]{:S(2)}, u32[]{:S(2)}) collective-permute-start(bf16[12,24,1024]{2,1,0:T(8,128)(2,1)S(1)} %get-tuple-element.214), channel_id=1, source_target_pairs={{0,16},{8,24},{16,32},{24,40},{32,48},{40,56},{48,64},{56,72},{64,... | collective-permute-start | bytes 1769480 | tf_op jit(solution)/shard_map/ppermute | solution.py:13
where the time goes:
time: 253 us; the launch traced here: 252 us
  waiting for transfers between devices  123 us (49%)
  blocking collectives  44.9 us (18%)
  starting transfers between devices  31.5 us (12%)
  matrix products  21 us (8%)
  local copies, waits for them, and re-layouts  19.6 us (8%)
  other arithmetic  11.2 us (4%)
    ppermute x2, waiting for transfers between devices, from_behind(): lax.ppermute(shard, axis, [(i, (i + by) % count) for i in range(count)])  103 us
    all_to_all x1, blocking collectives, several_exchanges(): lax.all_to_all(share, axis, split_axis=0, concat_axis=0, tiled=True)  25.5 us
    all_to_all x1, blocking collectives, body(): lax.all_to_all(row_fixed, 'head', split_axis=0, concat_axis=2, tiled=True)  19.3 us
    all_to_all x1, waiting for transfers between devices, several_exchanges(): lax.all_to_all(share, axis, split_axis=0, concat_axis=0, tiled=True)  19.1 us
    ppermute x2, starting transfers between devices, from_behind(): lax.ppermute(shard, axis, [(i, (i + by) % count) for i in range(count)])  16.3 us
    dot_general x8, matrix products, one_block(): jnp.einsum('qhd,khd->hqk', query_block, keys, preferred_element_type=jnp....  13.2 us
    dot_general x8, matrix products, one_block(): jnp.einsum('hqk,khd->qhd', weights.astype(jnp.bfloat16), values, preferre...  7.82 us
    all_to_all x1, starting transfers between devices, several_exchanges(): lax.all_to_all(share, axis, split_axis=0, concat_axis=0, tiled=True)  7.73 us
  transfers between devices with their start and end apart: 5, of which 4 were waited for; matrix products, arithmetic and copies ran while one was open for 3% of the time, Pallas kernels for 0%

commit v1 on v0

v1 whole, which is shorter than its diff:
```python
import math

import jax
import jax.numpy as jnp
from jax import lax
from jax.experimental import pallas as pl
from jax.experimental.pallas import tpu as pltpu
from jax.sharding import PartitionSpec as P

AXES = ("win", "head")
HEAD_DIM = 128
PEERS = 8


def flat(band, core, x, z_lo):
    return (band * 2 + core) * 8 + x * 2 + z_lo


def members(band, lat):
    out = []
    for late in range(2):
        if lat % 2 == 0:
            x, core = 1 + late, lat // 2
        else:
            x, core = (3, 0)[late], (lat // 2) ^ late
        for side in range(2):
            for z_lo in range(2):
                out.append(flat((band + side) % 32, core, x, z_lo))
    return out


def groups(parity):
    return [members(band, lat) for band in range(parity, 32, 2) for lat in range(4)]


def split_kernel(east_ref, qkv_ref, out_ref, sems):
    half = qkv_ref.shape[2] // 2
    first = pl.multiple_of(east_ref[0] * half, 8)
    copies = []
    for h in range(PEERS):
        copies.append(
            pltpu.make_async_copy(
                qkv_ref.at[:, :, pl.ds(first, half), h * HEAD_DIM : (h + 1) * HEAD_DIM],
                out_ref.at[h],
                sems.at[h],
            )
        )
    for copy in copies:
        copy.start()
    for copy in copies:
        copy.wait()


def split_heads(tokens, east):
    _, rows, cols, _ = tokens.shape
    return pl.pallas_call(
        split_kernel,
        out_shape=jax.ShapeDtypeStruct((PEERS, 3, rows, cols // 2, HEAD_DIM), tokens.dtype),
        in_specs=[
            pl.BlockSpec(memory_space=pltpu.SMEM),
            pl.BlockSpec(memory_space=pl.ANY),
        ],
        out_specs=pl.BlockSpec(memory_space=pl.ANY),
        scratch_shapes=[pltpu.SemaphoreType.DMA((PEERS,))],
        name="split_heads",
    )(east, tokens)


def join_kernel(east_ref, first_ref, second_ref, out_ref, sems):
    half = out_ref.shape[1] // 2
    copies = []
    for parity, blocks in enumerate((first_ref, second_ref)):
        east = east_ref[0] if parity == 0 else 1 - east_ref[0]
        col = pl.multiple_of(east * half, 8)
        for h in range(PEERS):
            copies.append(
                pltpu.make_async_copy(
                    blocks.at[h],
                    out_ref.at[:, pl.ds(col, half), h * HEAD_DIM : (h + 1) * HEAD_DIM],
                    sems.at[parity, h],
                )
            )
    for copy in copies:
        copy.start()
    for copy in copies:
        copy.wait()


def join_heads(east, first, second):
    heads, rows, half, width = first.shape
    return pl.pallas_call(
        join_kernel,
        out_shape=jax.ShapeDtypeStruct((rows, 2 * half, heads * width), first.dtype),
        in_specs=[
            pl.BlockSpec(memory_space=pltpu.SMEM),
            pl.BlockSpec(memory_space=pl.ANY),
            pl.BlockSpec(memory_space=pl.ANY),
        ],
        out_specs=pl.BlockSpec(memory_space=pl.ANY),
        scratch_shapes=[pltpu.SemaphoreType.DMA((2, PEERS))],
        name="join_heads",
    )(east, first, second)


def attend_kernel(split_ref, qkv_ref, out_ref, keys, values):
    blocks, _, count, width = qkv_ref.shape
    scale = 1.0 / math.sqrt(width)
    for b in range(blocks):
        keys[b * count : (b + 1) * count] = qkv_ref[b, 1]
        values[b * count : (b + 1) * count] = qkv_ref[b, 2]
    half = blocks // 2

    def attend(block, low, high):
        scores = lax.dot_general(
            qkv_ref[block, 0],
            keys[low:high],
            (((1,), (1,)), ((), ())),
            preferred_element_type=jnp.float32,
        )
        scores = scores * scale
        row_max = jnp.max(scores, axis=-1, keepdims=True)
        weights = jnp.exp(scores - row_max)
        row_total = jnp.sum(weights, axis=-1, keepdims=True)
        mixture = jnp.dot(
            weights.astype(jnp.bfloat16), values[low:high], preferred_element_type=jnp.float32
        )
        out_ref[block] = (mixture / row_total).astype(out_ref.dtype)

    @pl.when(split_ref[0] == 0)
    def _():
        for block in range(blocks):
            attend(block, 0, blocks * count)

    @pl.when(split_ref[0] != 0)
    def _():
        for block in range(blocks):
            low = 0 if block < half else half * count
            attend(block, low, low + half * count)


def attend(split, qkv):
    blocks, _, count, width = qkv.shape
    return pl.pallas_call(
        attend_kernel,
        out_shape=jax.ShapeDtypeStruct((blocks, count, width), qkv.dtype),
        in_specs=[
            pl.BlockSpec(memory_space=pltpu.SMEM),
            pl.BlockSpec(memory_space=pltpu.VMEM),
        ],
        out_specs=pl.BlockSpec(memory_space=pltpu.VMEM),
        scratch_shapes=[
            pltpu.VMEM((blocks * count, width), qkv.dtype),
            pltpu.VMEM((blocks * count, width), qkv.dtype),
        ],
        compiler_params=pltpu.CompilerParams(vmem_limit_bytes=48 * 2**20),
        name="attend",
    )(split, qkv)


def exchange(blocks, parity):
    return lax.all_to_all(
        blocks, AXES, split_axis=0, concat_axis=0, axis_index_groups=groups(parity), tiled=True
    )


def body(qkv):
    tokens = qkv[:, 0]
    rows, half = tokens.shape[1], tokens.shape[2] // 2
    win, head = lax.axis_index("win"), lax.axis_index("head")
    core, band_odd, x = win % 2, (win // 2) % 2, head // 2
    split = jnp.logical_or(
        jnp.logical_and(x == 3, core == 1), jnp.logical_and(x == 0, core == 0)
    ).astype(jnp.int32)[None]
    arrived = []
    for parity in (1, 0):
        east = (band_odd == parity).astype(jnp.int32)[None]
        arrived.append((parity, exchange(split_heads(tokens, east), parity)))
    outs = {}
    for parity, blocks in arrived:
        result = attend(split, blocks.reshape(PEERS, 3, rows * half, HEAD_DIM))
        outs[parity] = exchange(result.reshape(PEERS, rows, half, HEAD_DIM), parity)
    east_first = (band_odd == 0).astype(jnp.int32)[None]
    return join_heads(east_first, outs[0], outs[1])[None]


def solution(mesh):
    in_specs = (P(None, "win", "head", None, None),)
    out_specs = P("win", "head", None, None)
    return jax.shard_map(body, mesh=mesh, in_specs=in_specs, out_specs=out_specs, check_vma=False)
```

time: 253 us -> 240 us (0.949)
  Pallas kernels: 0 us -> 163 us
  waiting for transfers between devices: 123 us -> 25 us
  blocking collectives: 44.9 us -> 13.9 us
  matrix products: 21 us -> 0 us
  local copies, waits for them, and re-layouts: 19.6 us -> 0.81 us
  other arithmetic: 11.2 us -> 0 us
  starting transfers between devices: 31.5 us -> 36.2 us
    pallas_call x0 -> x5, Pallas kernels: none -> 163 us  [the longest x2 110 us: split_heads(): pl.pallas_call(split_kernel, out_shape=jax.ShapeDtypeStruct((PEERS, 3, ro...]
    ppermute x4 -> x0, waiting for transfers between devices: 104 us -> none  [the longest x2 103 us: from_behind(): lax.ppermute(shard, axis, [(i, (i + by) % count) for i in range(count)])]
    all_to_all x2 -> x1, blocking collectives: 44.9 us -> 13.9 us  [exchange(): lax.all_to_all(blocks, AXES, split_axis=0, concat_axis=0, axis_index_grou...]
    all_to_all x1 -> x3, starting transfers between devices: 7.73 us -> 36.2 us  [exchange(): lax.all_to_all(blocks, AXES, split_axis=0, concat_axis=0, axis_index_grou...]
    ppermute x4 -> x0, starting transfers between devices: 23.7 us -> none  [the longest x2 16.3 us: from_behind(): lax.ppermute(shard, axis, [(i, (i + by) % count) for i in range(count)])]
    dot_general x16 -> x0, matrix products: 21 us -> none  [the longest x8 13.2 us: one_block(): jnp.einsum('qhd,khd->hqk', query_block, keys, preferred_element_type=jnp....]
    reduce_sum x8 -> x0, other arithmetic: 6.92 us -> none  [one_block(): row_total = jnp.sum(weights, axis=-1, keepdims=True)]
    all_to_all x1 -> x3, waiting for transfers between devices: 19.1 us -> 25 us  [exchange(): lax.all_to_all(blocks, AXES, split_axis=0, concat_axis=0, axis_index_grou...]
  transfers between devices with their start and end apart: 5 -> 3, of which waited for: 4 -> 2; matrix products, arithmetic and copies ran while one was open for 3% -> 0% of each run, Pallas kernels for 0% -> 30%
where the time goes in v1:
time: 240 us; the launch traced here: 239 us
  Pallas kernels  163 us (68%)
  starting transfers between devices  36.2 us (15%)
  waiting for transfers between devices  25 us (10%)
  blocking collectives  13.9 us (6%)
    pallas_call x2, Pallas kernels, split_heads(): pl.pallas_call(split_kernel, out_shape=jax.ShapeDtypeStruct((PEERS, 3, ro...  110 us
    pallas_call x1, Pallas kernels, join_heads(): pl.pallas_call(join_kernel, out_shape=jax.ShapeDtypeStruct((rows, 2 * hal...  37 us
    all_to_all x3, starting transfers between devices, exchange(): lax.all_to_all(blocks, AXES, split_axis=0, concat_axis=0, axis_index_grou...  36.2 us
    all_to_all x3, waiting for transfers between devices, exchange(): lax.all_to_all(blocks, AXES, split_axis=0, concat_axis=0, axis_index_grou...  25 us
    pallas_call x2, Pallas kernels, attend(): pl.pallas_call(attend_kernel, out_shape=jax.ShapeDtypeStruct((blocks, cou...  16.7 us
    all_to_all x1, blocking collectives, exchange(): lax.all_to_all(blocks, AXES, split_axis=0, concat_axis=0, axis_index_grou...  13.9 us
  transfers between devices with their start and end apart: 3, of which 2 were waited for; matrix products, arithmetic and copies ran while one was open for 0% of the time, Pallas kernels for 30%

profile of v1, /device:TPU:1, one launch (start us, length us, event | category | flops | bytes accessed | tf_op | source)
XLA Modules:
  0.0 239.4 jit_solution(18230182492548735212)
XLA Ops:
  0.0 54.8 %split_heads.3 = bf16[8,3,12,24,128]{4,3,2,1,0:T(8,128)(2,1)} custom-call(s32[1]{0:T(128)} %bitcast.5.east_ref, bf16[3,12,48,1024]{3,2,1,0:T(8,128)(2,1)} %bitcast.13), custom_call_target="tpu_custom_call" | custom-call | tf_op jit(solution)/shard_map/split_heads/pallas_call | solution.py:56
  54.8 18.8 %all-to-all-start.2 = ((bf16[8,3,12,24,128]{4,3,2,1,0:T(8,128)(2,1)}), bf16[8,3,12,24,128]{4,3,2,1,0:T(8,128)(2,1)S(1)}, u32[]{:S(2)}, u32[]{:S(2)}) async-start(bf16[8,3,12,24,128]{4,3,2,1,0:T(8,128)(2,1)} %split_heads.3), calls=%async_computation.2 | async-start | bytes 3538944 | tf_op jit(solution)/shard_map/all_to_all | solution.py:161
  73.6 54.8 %split_heads.2 = bf16[8,3,12,24,128]{4,3,2,1,0:T(8,128)(2,1)} custom-call(s32[1]{0:T(128)} %bitcast.east_ref, bf16[3,12,48,1024]{3,2,1,0:T(8,128)(2,1)} %bitcast.14), custom_call_target="tpu_custom_call" | custom-call | tf_op jit(solution)/shard_map/split_heads/pallas_call | solution.py:56
  128.3 0.0 all-to-all-done.2
  128.4 5.1 %all-to-all-start = ((bf16[8,3,12,24,128]{4,3,2,1,0:T(8,128)(2,1)}), bf16[8,3,12,24,128]{4,3,2,1,0:T(8,128)(2,1)S(1)}, u32[]{:S(2)}, u32[]{:S(2)}) async-start(bf16[8,3,12,24,128]{4,3,2,1,0:T(8,128)(2,1)} %split_heads.2), calls=%async_computation | async-start | bytes 3538944 | tf_op jit(solution)/shard_map/all_to_all | solution.py:161
  133.5 8.2 %attend.3 = bf16[8,288,128]{2,1,0:T(8,128)(2,1)S(1)} custom-call(s32[1]{0:T(128)} %bitcast.1.split_ref, bf16[8,3,288,128]{3,2,1,0:T(8,128)(2,1)S(1)} %bitcast.9), custom_call_target="tpu_custom_call" | custom-call | tf_op jit(solution)/shard_map/attend/pallas_call | solution.py:143
  141.7 0.0 copy-start
  141.7 0.8 copy-done
  142.5 17.1 %all-to-all-done = bf16[8,3,12,24,128]{4,3,2,1,0:T(8,128)(2,1)S(1)} async-done(((bf16[8,3,12,24,128]{4,3,2,1,0:T(8,128)(2,1)}), bf16[8,3,12,24,128]{4,3,2,1,0:T(8,128)(2,1)S(1)}, u32[]{:S(2)}, u32[]{:S(2)}) %all-to-all-start) | async-done | bytes 1769504 | tf_op jit(solution)/shard_map/all_to_all | solution.py:161
  159.7 12.3 %all-to-all-start.3 = ((bf16[8,12,24,128]{3,2,1,0:T(8,128)(2,1)}), bf16[8,12,24,128]{3,2,1,0:T(8,128)(2,1)S(1)}, u32[]{:S(2)}, u32[]{:S(2)}) async-start(bf16[8,12,24,128]{3,2,1,0:T(8,128)(2,1)} %bitcast.11), calls=%async_computation.3 | async-start | bytes 1179648 | tf_op jit(solution)/shard_map/all_to_all | solution.py:161
  171.9 8.5 %attend.2 = bf16[8,288,128]{2,1,0:T(8,128)(2,1)S(1)} custom-call(s32[1]{0:T(128)} %bitcast.1.split_ref, bf16[8,3,288,128]{3,2,1,0:T(8,128)(2,1)S(1)} %bitcast.10), custom_call_target="tpu_custom_call" | custom-call | tf_op jit(solution)/shard_map/attend/pallas_call | solution.py:143
  180.4 7.9 %all-to-all-done.3.second_ref = bf16[8,12,24,128]{3,2,1,0:T(8,128)(2,1)S(1)} async-done(((bf16[8,12,24,128]{3,2,1,0:T(8,128)(2,1)}), bf16[8,12,24,128]{3,2,1,0:T(8,128)(2,1)S(1)}, u32[]{:S(2)}, u32[]{:S(2)}) %all-to-all-start.3) | async-done | bytes 589856 | tf_op jit(solution)/shard_map/all_to_all | solution.py:161
  188.3 0.0 copy-start.1
  188.3 13.9 %all_to_all.20.first_ref = bf16[8,12,24,128]{3,2,1,0:T(8,128)(2,1)} all-to-all(bf16[8,12,24,128]{3,2,1,0:T(8,128)(2,1)S(1)} %bitcast.12), channel_id=1, replica_groups={{2,3,18,19,4,5,20,21},{6,7,22,23,8,9,24,25},{10,11,26,27,12,13,28,29},{..., dimensions={0} | all-to-all | bytes 1179648 | tf_op jit(solution)/shard_map/all_to_all | solution.py:161
  202.2 0.0 copy-done.1
  202.2 37.0 %join_heads.1 = bf16[12,48,1024]{2,1,0:T(8,128)(2,1)} custom-call(s32[1]{0:T(128)} %bitcast.east_ref, bf16[8,12,24,128]{3,2,1,0:T(8,128)(2,1)} %all_to_all.20.first_ref, bf16[8,12,24,128]{3,2,1,0:T(8,128)(2,1)} %copy-done.1), custom_call_target="tpu_custom_call" | custom-call | tf_op jit(solution)/shard_map/join_heads/pallas_call | solution.py:91
Async XLA Ops:
  54.8 73.6 %all-to-all-start.2 = ((bf16[8,3,12,24,128]{4,3,2,1,0:T(8,128)(2,1)}), bf16[8,3,12,24,128]{4,3,2,1,0:T(8,128)(2,1)S(1)}, u32[]{:S(2)}, u32[]{:S(2)}) async-start(bf16[8,3,12,24,128]{4,3,2,1,0:T(8,128)(2,1)} %split_heads.3), calls=%async_computation.2 | async-start | bytes 3538944 | tf_op jit(solution)/shard_map/all_to_all | solution.py:161
  128.4 31.3 %all-to-all-start = ((bf16[8,3,12,24,128]{4,3,2,1,0:T(8,128)(2,1)}), bf16[8,3,12,24,128]{4,3,2,1,0:T(8,128)(2,1)S(1)}, u32[]{:S(2)}, u32[]{:S(2)}) async-start(bf16[8,3,12,24,128]{4,3,2,1,0:T(8,128)(2,1)} %split_heads.2), calls=%async_computation | async-start | bytes 3538944 | tf_op jit(solution)/shard_map/all_to_all | solution.py:161
  141.7 0.8 copy-start
  159.7 28.6 %all-to-all-start.3 = ((bf16[8,12,24,128]{3,2,1,0:T(8,128)(2,1)}), bf16[8,12,24,128]{3,2,1,0:T(8,128)(2,1)S(1)}, u32[]{:S(2)}, u32[]{:S(2)}) async-start(bf16[8,12,24,128]{3,2,1,0:T(8,128)(2,1)} %bitcast.11), calls=%async_computation.3 | async-start | bytes 1179648 | tf_op jit(solution)/shard_map/all_to_all | solution.py:161
  188.3 13.9 %copy-start.1 = (bf16[8,12,24,128]{3,2,1,0:T(8,128)(2,1)}, bf16[8,12,24,128]{3,2,1,0:T(8,128)(2,1)S(1)}, u32[]{:S(2)}) copy-start(bf16[8,12,24,128]{3,2,1,0:T(8,128)(2,1)S(1)} %all-to-all-done.3.second_ref) | copy-start | bytes 1769476

commit v2 on v0

v2 whole, which is shorter than its diff:
```python
import math

import jax
import jax.numpy as jnp
from jax import lax
from jax.experimental import pallas as pl
from jax.experimental.pallas import tpu as pltpu
from jax.sharding import PartitionSpec as P

AXES = ("win", "head")
HEAD_DIM = 128
PEERS = 8
SIDE = (0, 1, 4, 5)


def flat(band, core, x, z_lo):
    return (band % 32 * 2 + core) * 8 + x * 2 + z_lo


def place(lat, late):
    if lat % 2 == 0:
        return 1 + late, lat // 2
    return (3, 0)[late], (lat // 2) ^ late


def holders(band, lat):
    out = []
    for m in range(PEERS):
        x, core = place(lat, m >> 2)
        out.append(flat(band + (m >> 1 & 1), core, x, m & 1))
    return out


def workers(band, lat):
    if band % 8 != 7:
        return holders(band, lat)
    out = []
    for m in range(PEERS):
        x, core = place(lat, m >> 2)
        run = band // 8 + 1 - (m & 1)
        out.append(flat(run * 8 + (0 if m & 2 else 7), core, x, m & 1))
    return out


def windows(parity):
    return [(band, lat) for band in range(parity, 32, 2) for lat in range(4)]


def to_workers(parity, apart):
    return [
        (holders(*w)[m], workers(*w)[m ^ apart]) for w in windows(parity) for m in range(PEERS)
    ]


def to_holders(parity, apart):
    return [(worker, holder) for holder, worker in to_workers(parity, apart)]


def between_workers(parity, apart):
    return [
        (workers(*w)[m], workers(*w)[m ^ apart]) for w in windows(parity) for m in range(PEERS)
    ]


def exchange(blocks, parity):
    return lax.all_to_all(
        blocks,
        AXES,
        split_axis=0,
        concat_axis=0,
        axis_index_groups=[holders(*w) for w in windows(parity)],
        tiled=True,
    )


def lanes(h):
    start = h * HEAD_DIM
    return pl.ds(start if isinstance(h, int) else pl.multiple_of(start, HEAD_DIM), HEAD_DIM)


def split_even_kernel(east_ref, tokens_ref, out_ref):
    for h in range(PEERS):
        out_ref[h] = tokens_ref[..., lanes(h)]


def split_odd_kernel(where_ref, tokens_ref, *out_refs):
    for k, out_ref in enumerate(out_refs):
        out_ref[...] = tokens_ref[..., lanes(where_ref[1] ^ k)]


def split_even(tokens, east):
    kinds, rows, cols, channels = tokens.shape
    half = cols // 2
    return pl.pallas_call(
        split_even_kernel,
        out_shape=jax.ShapeDtypeStruct((PEERS, kinds, rows, half, HEAD_DIM), tokens.dtype),
        grid_spec=pltpu.PrefetchScalarGridSpec(
            num_scalar_prefetch=1,
            grid=(kinds,),
            in_specs=[pl.BlockSpec((1, rows, half, channels), lambda t, east: (t, 0, east[0], 0))],
            out_specs=pl.BlockSpec(
                (PEERS, 1, rows, half, HEAD_DIM), lambda t, east: (0, t, 0, 0, 0)
            ),
        ),
        name="split_even",
    )(east, tokens)


def split_odd(tokens, where):
    kinds, rows, cols, channels = tokens.shape
    half = cols // 2
    block = jax.ShapeDtypeStruct((kinds, rows, half, HEAD_DIM), tokens.dtype)
    return pl.pallas_call(
        split_odd_kernel,
        out_shape=[block] * PEERS,
        grid_spec=pltpu.PrefetchScalarGridSpec(
            num_scalar_prefetch=1,
            grid=(kinds,),
            in_specs=[
                pl.BlockSpec((1, rows, half, channels), lambda t, where: (t, 0, where[0], 0))
            ],
            out_specs=[pl.BlockSpec((1, rows, half, HEAD_DIM), lambda t, where: (t, 0, 0, 0))]
            * PEERS,
        ),
        name="split_odd",
    )(where, tokens)


def join_kernel(where_ref, even_ref, *refs):
    odd_refs, out_ref = refs[:-1], refs[-1]
    is_odd = pl.program_id(0) == where_ref[0]

    @pl.when(jnp.logical_not(is_odd))
    def _():
        for h in range(PEERS):
            out_ref[..., lanes(h)] = even_ref[h]

    @pl.when(is_odd)
    def _():
        for d, odd_ref in zip(SIDE, odd_refs):
            out_ref[..., lanes(where_ref[1] ^ d)] = odd_ref[0]
            out_ref[..., lanes(where_ref[1] ^ d ^ 2)] = odd_ref[1]


def join_heads(where, even, odd):
    heads, rows, half, width = even.shape

    def whole(shape):
        return pl.BlockSpec(shape, lambda c, where: (0,) * len(shape))

    return pl.pallas_call(
        join_kernel,
        out_shape=jax.ShapeDtypeStruct((rows, 2 * half, heads * width), even.dtype),
        grid_spec=pltpu.PrefetchScalarGridSpec(
            num_scalar_prefetch=1,
            grid=(2,),
            in_specs=[whole(even.shape)] + [whole(o.shape) for o in odd],
            out_specs=pl.BlockSpec((rows, half, heads * width), lambda c, where: (0, c, 0)),
        ),
        name="join_heads",
    )(where, even, *odd)


def attend_blocks(split_ref, blocks, outs, keys, values):
    count, width = blocks[0].shape[1:]
    scale = 1.0 / math.sqrt(width)
    for b, block in enumerate(blocks):
        keys[b * count : (b + 1) * count] = block[1]
        values[b * count : (b + 1) * count] = block[2]
    half = len(blocks) // 2

    def attend_one(b, low, high):
        scores = lax.dot_general(
            blocks[b][0],
            keys[low:high],
            (((1,), (1,)), ((), ())),
            preferred_element_type=jnp.float32,
        )
        scores = scores * scale
        row_max = jnp.max(scores, axis=-1, keepdims=True)
        weights = jnp.exp(scores - row_max)
        row_total = jnp.sum(weights, axis=-1, keepdims=True)
        mixture = jnp.dot(
            weights.astype(jnp.bfloat16), values[low:high], preferred_element_type=jnp.float32
        )
        outs[b][...] = (mixture / row_total).astype(outs[b].dtype)

    @pl.when(split_ref[0] == 0)
    def _():
        for b in range(len(blocks)):
            attend_one(b, 0, len(blocks) * count)

    @pl.when(split_ref[0] != 0)
    def _():
        for b in range(len(blocks)):
            low = 0 if b < half else half * count
            attend_one(b, low, low + half * count)


def attend_even_kernel(split_ref, qkv_ref, out_ref, keys, values):
    attend_blocks(
        split_ref,
        [qkv_ref.at[b] for b in range(PEERS)],
        [out_ref.at[b] for b in range(PEERS)],
        keys,
        values,
    )


def attend_odd_kernel(split_ref, *refs):
    blocks, (own_ref, other_ref, keys, values) = refs[:PEERS], refs[PEERS:]
    outs = [None] * PEERS
    for i, d in enumerate(SIDE):
        outs[d], outs[d ^ 2] = own_ref.at[i], other_ref.at[i]
    attend_blocks(split_ref, blocks, outs, keys, values)


def attend(kernel, name, split, operands, out_shape):
    count, width = operands[0].shape[-2:]
    vmem = pl.BlockSpec(memory_space=pltpu.VMEM)
    return pl.pallas_call(
        kernel,
        out_shape=out_shape,
        in_specs=[pl.BlockSpec(memory_space=pltpu.SMEM)] + [vmem] * len(operands),
        out_specs=jax.tree.map(lambda _: vmem, out_shape),
        scratch_shapes=[pltpu.VMEM((PEERS * count, width), operands[0].dtype)] * 2,
        compiler_params=pltpu.CompilerParams(vmem_limit_bytes=48 * 2**20),
        name=name,
    )(split, *operands)


def body(qkv):
    tokens = qkv[:, 0]
    rows, half = tokens.shape[1], tokens.shape[2] // 2
    count = rows * half
    win, head = lax.axis_index("win"), lax.axis_index("head")
    core, band_odd, x, z_lo = win & 1, (win >> 1) & 1, head >> 1, head & 1
    late = ((x == 2) | (x == 0)).astype(jnp.int32)
    member = late * 4 + (1 - band_odd) * 2 + z_lo
    where = jnp.stack([band_odd, member])
    east = (1 - band_odd)[None]
    split = (((x == 3) & (core == 1)) | ((x == 0) & (core == 0))).astype(jnp.int32)[None]

    even = exchange(split_even(tokens, east), 0)
    odd = split_odd(tokens, where)
    odd = [lax.ppermute(odd[k], AXES, to_workers(1, k)) for k in range(PEERS)]

    result = attend(
        attend_even_kernel,
        "attend_even",
        split,
        [even.reshape(PEERS, 3, count, HEAD_DIM)],
        jax.ShapeDtypeStruct((PEERS, count, HEAD_DIM), qkv.dtype),
    )
    even = exchange(result.reshape(PEERS, rows, half, HEAD_DIM), 0)

    own, other = attend(
        attend_odd_kernel,
        "attend_odd",
        split,
        [o.reshape(3, count, HEAD_DIM) for o in odd],
        [jax.ShapeDtypeStruct((4, count, HEAD_DIM), qkv.dtype)] * 2,
    )
    other = lax.ppermute(other, AXES, between_workers(1, 2))
    odd = []
    for i, d in enumerate(SIDE):
        pair = jnp.stack([own[i], other[i]]).reshape(2, rows, half, HEAD_DIM)
        odd.append(lax.ppermute(pair, AXES, to_holders(1, d)))
    return join_heads(where, even, odd)[None]


def solution(mesh):
    in_specs = (P(None, "win", "head", None, None),)
    out_specs = P("win", "head", None, None)
    return jax.shard_map(body, mesh=mesh, in_specs=in_specs, out_specs=out_specs, check_vma=False)
```

time: 253 us -> 129 us (0.51)
  waiting for transfers between devices: 123 us -> 15.9 us
  starting transfers between devices: 31.5 us -> 78 us
  blocking collectives: 44.9 us -> 0 us
  Pallas kernels: 0 us -> 30.4 us
  matrix products: 21 us -> 0 us
  local copies, waits for them, and re-layouts: 19.6 us -> 3.14 us
  other arithmetic: 11.2 us -> 0.74 us
    ppermute x4 -> x13, waiting for transfers between devices: 104 us -> 15.9 us  [the longest x8 8.04 us: body(): odd = [lax.ppermute(odd[k], AXES, to_workers(1, k)) for k in range(PEERS)]]
    all_to_all x2 -> x0, blocking collectives: 44.9 us -> none  [the longest x1 25.5 us: several_exchanges(): lax.all_to_all(share, axis, split_axis=0, concat_axis=0, tiled=True)]
    ppermute x4 -> x13, starting transfers between devices: 23.7 us -> 61.3 us  [the longest x8 45.5 us: body(): odd = [lax.ppermute(odd[k], AXES, to_workers(1, k)) for k in range(PEERS)]]
    pallas_call x0 -> x5, Pallas kernels: none -> 30.4 us  [the longest x2 19.3 us: attend(): pl.pallas_call(kernel, out_shape=out_shape, in_specs=[pl.BlockSpec(memory...]
    dot_general x16 -> x0, matrix products: 21 us -> none  [the longest x8 13.2 us: one_block(): jnp.einsum('qhd,khd->hqk', query_block, keys, preferred_element_type=jnp....]
    all_to_all x1 -> x2, waiting for transfers between devices: 19.1 us -> 0.01 us  [exchange(): lax.all_to_all(blocks, AXES, split_axis=0, concat_axis=0, axis_index_grou...]
    all_to_all x1 -> x2, starting transfers between devices: 7.73 us -> 16.7 us  [exchange(): lax.all_to_all(blocks, AXES, split_axis=0, concat_axis=0, axis_index_grou...]
    reduce_sum x8 -> x0, other arithmetic: 6.92 us -> none  [one_block(): row_total = jnp.sum(weights, axis=-1, keepdims=True)]
  transfers between devices with their start and end apart: 5 -> 15, of which waited for: 4 -> 4; matrix products, arithmetic and copies ran while one was open for 3% -> 1% of each run, Pallas kernels for 0% -> 18%
where the time goes in v2:
time: 129 us; the launch traced here: 128 us
  starting transfers between devices  78 us (60%)
  Pallas kernels  30.4 us (24%)
  waiting for transfers between devices  15.9 us (12%)
  local copies, waits for them, and re-layouts  3.14 us (2%)
    ppermute x8, starting transfers between devices, body(): odd = [lax.ppermute(odd[k], AXES, to_workers(1, k)) for k in range(PEERS)]  45.5 us
    pallas_call x2, Pallas kernels, attend(): pl.pallas_call(kernel, out_shape=out_shape, in_specs=[pl.BlockSpec(memory...  19.3 us
    all_to_all x2, starting transfers between devices, exchange(): lax.all_to_all(blocks, AXES, split_axis=0, concat_axis=0, axis_index_grou...  16.7 us
    ppermute x4, starting transfers between devices, body(): odd.append(lax.ppermute(pair, AXES, to_holders(1, d)))  9.66 us
    ppermute x8, waiting for transfers between devices, body(): odd = [lax.ppermute(odd[k], AXES, to_workers(1, k)) for k in range(PEERS)]  8.04 us
    ppermute x4, waiting for transfers between devices, body(): odd.append(lax.ppermute(pair, AXES, to_holders(1, d)))  7.83 us
    ppermute x1, starting transfers between devices, body(): other = lax.ppermute(other, AXES, between_workers(1, 2))  6.09 us
    pallas_call x1, Pallas kernels, split_odd(): pl.pallas_call(split_odd_kernel, out_shape=[block] * PEERS, grid_spec=plt...  4.37 us
  transfers between devices with their start and end apart: 15, of which 4 were waited for; matrix products, arithmetic and copies ran while one was open for 1% of the time, Pallas kernels for 18%

profile of v2, /device:TPU:1, one launch (start us, length us, event | category | flops | bytes accessed | tf_op | source)
XLA Modules:
  0.0 128.4 jit_solution(16654209275246515032)
XLA Ops:
  0.0 3.6 %split_even.1 = bf16[8,3,12,24,128]{4,3,2,1,0:T(8,128)(2,1)} custom-call(s32[1]{0:T(128)} %bitcast.3.east_ref, bf16[3,12,48,1024]{3,2,1,0:T(8,128)(2,1)} %bitcast.28), custom_call_target="tpu_custom_call" | custom-call | tf_op jit(solution)/shard_map/split_even/pallas_call | solution.py:94
  3.6 8.5 %all-to-all-start = ((bf16[8,3,12,24,128]{4,3,2,1,0:T(8,128)(2,1)}), bf16[8,3,12,24,128]{4,3,2,1,0:T(8,128)(2,1)S(1)}, u32[]{:S(2)}, u32[]{:S(2)}) async-start(bf16[8,3,12,24,128]{4,3,2,1,0:T(8,128)(2,1)} %split_even.1), calls=%async_computation | async-start | bytes 3538944 | tf_op jit(solution)/shard_map/all_to_all | solution.py:66
  12.2 0.7 pad_add_fusion.where_ref
  12.8 4.4 %split_odd.1 = (bf16[3,12,24,128]{3,2,1,0:T(8,128)(2,1)}, bf16[3,12,24,128]{3,2,1,0:T(8,128)(2,1)}, bf16[3,12,24,128]{3,2,1,0:T(8,128)(2,1)}, bf16[3,12,24,128]{...) custom-call(s32[2]{0:T(128)} %pad_add_fusion.where_ref, ...), custom_call_target="tpu_custom_call" | custom-call | tf_op jit(solution)/shard_map/split_odd/pallas_call | solution.py:113
  17.2 1.6 %collective-permute-start = (bf16[3,12,24,128]{3,2,1,0:T(8,128)(2,1)}, bf16[3,12,24,128]{3,2,1,0:T(8,128)(2,1)S(1)}, u32[]{:S(2)}, u32[]{:S(2)}) collective-permute-start(bf16[3,12,24,128]{3,2,1,0:T(8,128)(2,1)} %get-tuple-element.15), channel_id=1, source_target_pairs={{18,18},{19,19},{34,34},{35,35},{20,20},{21,21},{36,36},{37,37},{2... | collective-permute-start | bytes 663560 | tf_op jit(solution)/shard_map/ppermute | solution.py:246
  18.8 10.3 %collective-permute-start.1 = (bf16[3,12,24,128]{3,2,1,0:T(8,128)(2,1)}, bf16[3,12,24,128]{3,2,1,0:T(8,128)(2,1)S(1)}, u32[]{:S(2)}, u32[]{:S(2)}) collective-permute-start(bf16[3,12,24,128]{3,2,1,0:T(8,128)(2,1)} %get-tuple-element.16), channel_id=1, source_target_pairs={{18,19},{19,18},{34,35},{35,34},{20,21},{21,20},{36,37},{37,36},{2... | collective-permute-start | bytes 663560 | tf_op jit(solution)/shard_map/ppermute | solution.py:246
  29.1 1.9 %collective-permute-start.2 = (bf16[3,12,24,128]{3,2,1,0:T(8,128)(2,1)}, bf16[3,12,24,128]{3,2,1,0:T(8,128)(2,1)S(1)}, u32[]{:S(2)}, u32[]{:S(2)}) collective-permute-start(bf16[3,12,24,128]{3,2,1,0:T(8,128)(2,1)} %get-tuple-element.17), channel_id=1, source_target_pairs={{18,34},{19,35},{34,18},{35,19},{20,36},{21,37},{36,20},{37,21},{2... | collective-permute-start | bytes 663560 | tf_op jit(solution)/shard_map/ppermute | solution.py:246
  31.0 4.8 %collective-permute-start.3 = (bf16[3,12,24,128]{3,2,1,0:T(8,128)(2,1)}, bf16[3,12,24,128]{3,2,1,0:T(8,128)(2,1)S(1)}, u32[]{:S(2)}, u32[]{:S(2)}) collective-permute-start(bf16[3,12,24,128]{3,2,1,0:T(8,128)(2,1)} %get-tuple-element.18), channel_id=1, source_target_pairs={{18,35},{19,34},{34,19},{35,18},{20,37},{21,36},{36,21},{37,20},{2... | collective-permute-start | bytes 663560 | tf_op jit(solution)/shard_map/ppermute | solution.py:246
  35.9 2.8 %collective-permute-start.4 = (bf16[3,12,24,128]{3,2,1,0:T(8,128)(2,1)}, bf16[3,12,24,128]{3,2,1,0:T(8,128)(2,1)S(1)}, u32[]{:S(2)}, u32[]{:S(2)}) collective-permute-start(bf16[3,12,24,128]{3,2,1,0:T(8,128)(2,1)} %get-tuple-element.19), channel_id=1, source_target_pairs={{18,20},{19,21},{34,36},{35,37},{20,18},{21,19},{36,34},{37,35},{2... | collective-permute-start | bytes 663560 | tf_op jit(solution)/shard_map/ppermute | solution.py:246
  38.7 0.0 collective-permute-done
  38.7 8.8 %collective-permute-start.5 = (bf16[3,12,24,128]{3,2,1,0:T(8,128)(2,1)}, bf16[3,12,24,128]{3,2,1,0:T(8,128)(2,1)S(1)}, u32[]{:S(2)}, u32[]{:S(2)}) collective-permute-start(bf16[3,12,24,128]{3,2,1,0:T(8,128)(2,1)} %get-tuple-element.20), channel_id=1, source_target_pairs={{18,21},{19,20},{34,37},{35,36},{20,19},{21,18},{36,35},{37,34},{2... | collective-permute-start | bytes 663560 | tf_op jit(solution)/shard_map/ppermute | solution.py:246
  47.5 0.0 collective-permute-done.1
  47.5 7.3 %collective-permute-start.6 = (bf16[3,12,24,128]{3,2,1,0:T(8,128)(2,1)}, bf16[3,12,24,128]{3,2,1,0:T(8,128)(2,1)S(1)}, u32[]{:S(2)}, u32[]{:S(2)}) collective-permute-start(bf16[3,12,24,128]{3,2,1,0:T(8,128)(2,1)} %get-tuple-element.21), channel_id=1, source_target_pairs={{18,36},{19,37},{34,20},{35,21},{20,34},{21,35},{36,18},{37,19},{2... | collective-permute-start | bytes 663560 | tf_op jit(solution)/shard_map/ppermute | solution.py:246
  54.8 0.0 collective-permute-done.2
  54.8 8.0 %collective-permute-start.7 = (bf16[3,12,24,128]{3,2,1,0:T(8,128)(2,1)}, bf16[3,12,24,128]{3,2,1,0:T(8,128)(2,1)}, u32[]{:S(2)}, u32[]{:S(2)}) collective-permute-start(bf16[3,12,24,128]{3,2,1,0:T(8,128)(2,1)} %get-tuple-element.22), channel_id=1, source_target_pairs={{18,37},{19,36},{34,21},{35,20},{20,35},{21,34},{36,19},{37,18},{2... | collective-permute-start | bytes 663560 | tf_op jit(solution)/shard_map/ppermute | solution.py:246
  62.8 0.0 collective-permute-done.3
  62.8 0.0 collective-permute-done.4
  62.8 0.0 collective-permute-done.5
  62.8 1.0 collective-permute-done.6
  63.8 0.7 copy-done
  64.5 7.0 %collective-permute-done.7 = bf16[3,12,24,128]{3,2,1,0:T(8,128)(2,1)} collective-permute-done((bf16[3,12,24,128]{3,2,1,0:T(8,128)(2,1)}, bf16[3,12,24,128]{3,2,1,0:T(8,128)(2,1)}, u32[]{:S(2)}, u32[]{:S(2)}) %collective-permute-start.7) | collective-permute-done | bytes 221216 | tf_op jit(solution)/shard_map/ppermute | solution.py:246
  71.5 0.0 copy-start.1
  71.5 0.9 copy-done.1
  72.5 10.0 %attend_odd.1 = (bf16[4,288,128]{2,1,0:T(8,128)(2,1)S(1)}, bf16[4,288,128]{2,1,0:T(8,128)(2,1)}) custom-call(s32[1]{0:T(128)} %bitcast.2.split_ref, bf16[3,288,128]{2,1,0:T(8,128)(2,1)S(1)} %bitcast.21, bf16[3,288,128]{2,1,0:T(8,128)(2,1)S(1)} %bitcast.22, bf16[3,288,128]{2,1,0:T(8,128)(2,1)S(1)} %bitcast.23, bf16[3,288,128]{2,1,0:T(8,128)(2,1)S(1)} %bitcast.24, ...), custom_call_target="tpu_custom_call" | custom-call | tf_op jit(solution)/shard_map/attend_odd/pallas_call | solution.py:221
  82.4 6.1 %collective-permute-start.8 = (bf16[4,288,128]{2,1,0:T(8,128)(2,1)}, bf16[4,288,128]{2,1,0:T(8,128)(2,1)S(1)}, u32[]{:S(2)}, u32[]{:S(2)}) collective-permute-start(bf16[4,288,128]{2,1,0:T(8,128)(2,1)} %get-tuple-element.24), channel_id=1, source_target_pairs={{18,34},{19,35},{34,18},{35,19},{20,36},{21,37},{36,20},{37,21},{2... | collective-permute-start | bytes 884744 | tf_op jit(solution)/shard_map/ppermute | solution.py:264
  88.5 0.0 all-to-all-done
  88.5 9.3 %attend_even.1 = bf16[8,288,128]{2,1,0:T(8,128)(2,1)} custom-call(s32[1]{0:T(128)} %bitcast.2.split_ref, bf16[8,3,288,128]{3,2,1,0:T(8,128)(2,1)S(1)} %bitcast.20), custom_call_target="tpu_custom_call" | custom-call | tf_op jit(solution)/shard_map/attend_even/pallas_call | solution.py:221
  97.9 8.2 %all-to-all-start.1 = ((bf16[8,12,24,128]{3,2,1,0:T(8,128)(2,1)}), bf16[8,12,24,128]{3,2,1,0:T(8,128)(2,1)S(1)}, u32[]{:S(2)}, u32[]{:S(2)}) async-start(bf16[8,12,24,128]{3,2,1,0:T(8,128)(2,1)} %bitcast.6), calls=%async_computation.1 | async-start | bytes 1179648 | tf_op jit(solution)/shard_map/all_to_all | solution.py:66
  106.1 0.0 collective-permute-done.8
  106.1 0.7 collective-permute-start.9
  106.8 4.3 %collective-permute-start.10 = (bf16[2,12,24,128]{3,2,1,0:T(8,128)(2,1)S(1)}, bf16[2,12,24,128]{3,2,1,0:T(8,128)(2,1)S(1)}, u32[]{:S(2)}, u32[]{:S(2)}) collective-permute-start(bf16[2,12,24,128]{3,2,1,0:T(8,128)(2,1)S(1)} %bitcast.31), channel_id=1, source_target_pairs={{19,18},{18,19},{35,34},{34,35},{21,20},{20,21},{37,36},{36,37},{2... | collective-permute-start | bytes 442376 | tf_op jit(solution)/shard_map/ppermute | solution.py:268
  111.2 2.7 %collective-permute-start.11 = (bf16[2,12,24,128]{3,2,1,0:T(8,128)(2,1)S(1)}, bf16[2,12,24,128]{3,2,1,0:T(8,128)(2,1)S(1)}, u32[]{:S(2)}, u32[]{:S(2)}) collective-permute-start(bf16[2,12,24,128]{3,2,1,0:T(8,128)(2,1)S(1)} %bitcast.32), channel_id=1, source_target_pairs={{20,18},{21,19},{36,34},{37,35},{18,20},{19,21},{34,36},{35,37},{2... | collective-permute-start | bytes 442376 | tf_op jit(solution)/shard_map/ppermute | solution.py:268
  114.0 1.9 %collective-permute-start.12 = (bf16[2,12,24,128]{3,2,1,0:T(8,128)(2,1)S(1)}, bf16[2,12,24,128]{3,2,1,0:T(8,128)(2,1)S(1)}, u32[]{:S(2)}, u32[]{:S(2)}) collective-permute-start(bf16[2,12,24,128]{3,2,1,0:T(8,128)(2,1)S(1)} %bitcast.33), channel_id=1, source_target_pairs={{21,18},{20,19},{37,34},{36,35},{19,20},{18,21},{35,36},{34,37},{2... | collective-permute-start | bytes 442376 | tf_op jit(solution)/shard_map/ppermute | solution.py:268
  115.9 0.0 collective-permute-done.9.refs_0_
  115.9 0.0 copy-start.3
  115.9 4.9 %collective-permute-done.10.refs_1_ = bf16[2,12,24,128]{3,2,1,0:T(8,128)(2,1)S(1)} collective-permute-done((bf16[2,12,24,128]{3,2,1,0:T(8,128)(2,1)S(1)}, bf16[2,12,24,128]{3,2,1,0:T(8,128)(2,1)S(1)}, u32[]{:S(2)}, u32[]{:S(2)}) %collective-permute-start.10) | collective-permute-done | bytes 147488 | tf_op jit(solution)/shard_map/ppermute | solution.py:268
  120.8 0.0 copy-start.4
  120.8 0.0 collective-permute-done.11.refs_2_
  120.9 0.0 copy-start.5
  120.9 2.9 %collective-permute-done.12.refs_3_ = bf16[2,12,24,128]{3,2,1,0:T(8,128)(2,1)S(1)} collective-permute-done((bf16[2,12,24,128]{3,2,1,0:T(8,128)(2,1)S(1)}, bf16[2,12,24,128]{3,2,1,0:T(8,128)(2,1)S(1)}, u32[]{:S(2)}, u32[]{:S(2)}) %collective-permute-start.12) | collective-permute-done | bytes 147488 | tf_op jit(solution)/shard_map/ppermute | solution.py:268
  123.7 0.0 copy-start.6
  123.7 0.0 all-to-all-done.1.even_ref
  123.8 0.0 copy-done.3
  123.8 0.0 copy-done.4
  123.8 0.0 copy-done.5
  123.8 0.6 copy-done.6
  124.4 0.8 copy-done.2
  125.2 3.2 %join_heads.1 = bf16[12,48,1024]{2,1,0:T(8,128)(2,1)} custom-call(s32[2]{0:T(128)} %pad_add_fusion.where_ref, bf16[8,12,24,128]{3,2,1,0:T(8,128)(2,1)} %copy-done.2, bf16[2,12,24,128]{3,2,1,0:T(8,128)(2,1)} %copy-done.3, bf16[2,12,24,128]{3,2,1,0:T(8,128)(2,1)} %copy-done.4, bf16[2,12,24,128]{3,2,1,0:T(8,128)(2,1)} %copy-done.5, ...), custom_call_target="tpu_custom_call" | custom-call | tf_op jit(solution)/shard_map/join_heads/pallas_call | solution.py:151
  (8 shorter events, 0.1 us)
Async XLA Ops:
  3.6 84.9 %all-to-all-start = ((bf16[8,3,12,24,128]{4,3,2,1,0:T(8,128)(2,1)}), bf16[8,3,12,24,128]{4,3,2,1,0:T(8,128)(2,1)S(1)}, u32[]{:S(2)}, u32[]{:S(2)}) async-start(bf16[8,3,12,24,128]{4,3,2,1,0:T(8,128)(2,1)} %split_even.1), calls=%async_computation | async-start | bytes 3538944 | tf_op jit(solution)/shard_map/all_to_all | solution.py:66
  17.2 21.5 %collective-permute-start = (bf16[3,12,24,128]{3,2,1,0:T(8,128)(2,1)}, bf16[3,12,24,128]{3,2,1,0:T(8,128)(2,1)S(1)}, u32[]{:S(2)}, u32[]{:S(2)}) collective-permute-start(bf16[3,12,24,128]{3,2,1,0:T(8,128)(2,1)} %get-tuple-element.15), channel_id=1, source_target_pairs={{18,18},{19,19},{34,34},{35,35},{20,20},{21,21},{36,36},{37,37},{2... | collective-permute-start | bytes 663560 | tf_op jit(solution)/shard_map/ppermute | solution.py:246
  18.8 28.7 %collective-permute-start.1 = (bf16[3,12,24,128]{3,2,1,0:T(8,128)(2,1)}, bf16[3,12,24,128]{3,2,1,0:T(8,128)(2,1)S(1)}, u32[]{:S(2)}, u32[]{:S(2)}) collective-permute-start(bf16[3,12,24,128]{3,2,1,0:T(8,128)(2,1)} %get-tuple-element.16), channel_id=1, source_target_pairs={{18,19},{19,18},{34,35},{35,34},{20,21},{21,20},{36,37},{37,36},{2... | collective-permute-start | bytes 663560 | tf_op jit(solution)/shard_map/ppermute | solution.py:246
  29.1 25.6 %collective-permute-start.2 = (bf16[3,12,24,128]{3,2,1,0:T(8,128)(2,1)}, bf16[3,12,24,128]{3,2,1,0:T(8,128)(2,1)S(1)}, u32[]{:S(2)}, u32[]{:S(2)}) collective-permute-start(bf16[3,12,24,128]{3,2,1,0:T(8,128)(2,1)} %get-tuple-element.17), channel_id=1, source_target_pairs={{18,34},{19,35},{34,18},{35,19},{20,36},{21,37},{36,20},{37,21},{2... | collective-permute-start | bytes 663560 | tf_op jit(solution)/shard_map/ppermute | solution.py:246
  31.0 31.7 %collective-permute-start.3 = (bf16[3,12,24,128]{3,2,1,0:T(8,128)(2,1)}, bf16[3,12,24,128]{3,2,1,0:T(8,128)(2,1)S(1)}, u32[]{:S(2)}, u32[]{:S(2)}) collective-permute-start(bf16[3,12,24,128]{3,2,1,0:T(8,128)(2,1)} %get-tuple-element.18), channel_id=1, source_target_pairs={{18,35},{19,34},{34,19},{35,18},{20,37},{21,36},{36,21},{37,20},{2... | collective-permute-start | bytes 663560 | tf_op jit(solution)/shard_map/ppermute | solution.py:246
  35.9 26.9 %collective-permute-start.4 = (bf16[3,12,24,128]{3,2,1,0:T(8,128)(2,1)}, bf16[3,12,24,128]{3,2,1,0:T(8,128)(2,1)S(1)}, u32[]{:S(2)}, u32[]{:S(2)}) collective-permute-start(bf16[3,12,24,128]{3,2,1,0:T(8,128)(2,1)} %get-tuple-element.19), channel_id=1, source_target_pairs={{18,20},{19,21},{34,36},{35,37},{20,18},{21,19},{36,34},{37,35},{2... | collective-permute-start | bytes 663560 | tf_op jit(solution)/shard_map/ppermute | solution.py:246
  38.7 24.1 %collective-permute-start.5 = (bf16[3,12,24,128]{3,2,1,0:T(8,128)(2,1)}, bf16[3,12,24,128]{3,2,1,0:T(8,128)(2,1)S(1)}, u32[]{:S(2)}, u32[]{:S(2)}) collective-permute-start(bf16[3,12,24,128]{3,2,1,0:T(8,128)(2,1)} %get-tuple-element.20), channel_id=1, source_target_pairs={{18,21},{19,20},{34,37},{35,36},{20,19},{21,18},{36,35},{37,34},{2... | collective-permute-start | bytes 663560 | tf_op jit(solution)/shard_map/ppermute | solution.py:246
  47.5 16.4 %collective-permute-start.6 = (bf16[3,12,24,128]{3,2,1,0:T(8,128)(2,1)}, bf16[3,12,24,128]{3,2,1,0:T(8,128)(2,1)S(1)}, u32[]{:S(2)}, u32[]{:S(2)}) collective-permute-start(bf16[3,12,24,128]{3,2,1,0:T(8,128)(2,1)} %get-tuple-element.21), channel_id=1, source_target_pairs={{18,36},{19,37},{34,20},{35,21},{20,34},{21,35},{36,18},{37,19},{2... | collective-permute-start | bytes 663560 | tf_op jit(solution)/shard_map/ppermute | solution.py:246
  54.8 16.8 %collective-permute-start.7 = (bf16[3,12,24,128]{3,2,1,0:T(8,128)(2,1)}, bf16[3,12,24,128]{3,2,1,0:T(8,128)(2,1)}, u32[]{:S(2)}, u32[]{:S(2)}) collective-permute-start(bf16[3,12,24,128]{3,2,1,0:T(8,128)(2,1)} %get-tuple-element.22), channel_id=1, source_target_pairs={{18,37},{19,36},{34,21},{35,20},{20,35},{21,34},{36,19},{37,18},{2... | collective-permute-start | bytes 663560 | tf_op jit(solution)/shard_map/ppermute | solution.py:246
  63.8 0.7 copy-start
  71.5 0.9 copy-start.1
  82.4 23.6 %collective-permute-start.8 = (bf16[4,288,128]{2,1,0:T(8,128)(2,1)}, bf16[4,288,128]{2,1,0:T(8,128)(2,1)S(1)}, u32[]{:S(2)}, u32[]{:S(2)}) collective-permute-start(bf16[4,288,128]{2,1,0:T(8,128)(2,1)} %get-tuple-element.24), channel_id=1, source_target_pairs={{18,34},{19,35},{34,18},{35,19},{20,36},{21,37},{36,20},{37,21},{2... | collective-permute-start | bytes 884744 | tf_op jit(solution)/shard_map/ppermute | solution.py:264
  97.9 25.9 %all-to-all-start.1 = ((bf16[8,12,24,128]{3,2,1,0:T(8,128)(2,1)}), bf16[8,12,24,128]{3,2,1,0:T(8,128)(2,1)S(1)}, u32[]{:S(2)}, u32[]{:S(2)}) async-start(bf16[8,12,24,128]{3,2,1,0:T(8,128)(2,1)} %bitcast.6), calls=%async_computation.1 | async-start | bytes 1179648 | tf_op jit(solution)/shard_map/all_to_all | solution.py:66
  106.1 9.8 %collective-permute-start.9 = (bf16[2,12,24,128]{3,2,1,0:T(8,128)(2,1)S(1)}, bf16[2,12,24,128]{3,2,1,0:T(8,128)(2,1)S(1)}, u32[]{:S(2)}, u32[]{:S(2)}) collective-permute-start(bf16[2,12,24,128]{3,2,1,0:T(8,128)(2,1)S(1)} %bitcast.30), channel_id=1, source_target_pairs={{18,18},{19,19},{34,34},{35,35},{20,20},{21,21},{36,36},{37,37},{2... | collective-permute-start | bytes 442376 | tf_op jit(solution)/shard_map/ppermute | solution.py:268
  106.8 14.0 %collective-permute-start.10 = (bf16[2,12,24,128]{3,2,1,0:T(8,128)(2,1)S(1)}, bf16[2,12,24,128]{3,2,1,0:T(8,128)(2,1)S(1)}, u32[]{:S(2)}, u32[]{:S(2)}) collective-permute-start(bf16[2,12,24,128]{3,2,1,0:T(8,128)(2,1)S(1)} %bitcast.31), channel_id=1, source_target_pairs={{19,18},{18,19},{35,34},{34,35},{21,20},{20,21},{37,36},{36,37},{2... | collective-permute-start | bytes 442376 | tf_op jit(solution)/shard_map/ppermute | solution.py:268
  111.2 9.6 %collective-permute-start.11 = (bf16[2,12,24,128]{3,2,1,0:T(8,128)(2,1)S(1)}, bf16[2,12,24,128]{3,2,1,0:T(8,128)(2,1)S(1)}, u32[]{:S(2)}, u32[]{:S(2)}) collective-permute-start(bf16[2,12,24,128]{3,2,1,0:T(8,128)(2,1)S(1)} %bitcast.32), channel_id=1, source_target_pairs={{20,18},{21,19},{36,34},{37,35},{18,20},{19,21},{34,36},{35,37},{2... | collective-permute-start | bytes 442376 | tf_op jit(solution)/shard_map/ppermute | solution.py:268
  114.0 9.8 %collective-permute-start.12 = (bf16[2,12,24,128]{3,2,1,0:T(8,128)(2,1)S(1)}, bf16[2,12,24,128]{3,2,1,0:T(8,128)(2,1)S(1)}, u32[]{:S(2)}, u32[]{:S(2)}) collective-permute-start(bf16[2,12,24,128]{3,2,1,0:T(8,128)(2,1)S(1)} %bitcast.33), channel_id=1, source_target_pairs={{21,18},{20,19},{37,34},{36,35},{19,20},{18,21},{35,36},{34,37},{2... | collective-permute-start | bytes 442376 | tf_op jit(solution)/shard_map/ppermute | solution.py:268
  115.9 7.9 %copy-start.3 = (bf16[2,12,24,128]{3,2,1,0:T(8,128)(2,1)}, bf16[2,12,24,128]{3,2,1,0:T(8,128)(2,1)S(1)}, u32[]{:S(2)}) copy-start(bf16[2,12,24,128]{3,2,1,0:T(8,128)(2,1)S(1)} %collective-permute-done.9.refs_0_) | copy-start | bytes 442372
  120.8 2.9 %copy-start.4 = (bf16[2,12,24,128]{3,2,1,0:T(8,128)(2,1)}, bf16[2,12,24,128]{3,2,1,0:T(8,128)(2,1)S(1)}, u32[]{:S(2)}) copy-start(bf16[2,12,24,128]{3,2,1,0:T(8,128)(2,1)S(1)} %collective-permute-done.10.refs_1_) | copy-start | bytes 442372
  120.9 2.9 %copy-start.5 = (bf16[2,12,24,128]{3,2,1,0:T(8,128)(2,1)}, bf16[2,12,24,128]{3,2,1,0:T(8,128)(2,1)S(1)}, u32[]{:S(2)}) copy-start(bf16[2,12,24,128]{3,2,1,0:T(8,128)(2,1)S(1)} %collective-permute-done.11.refs_2_) | copy-start | bytes 442372
  123.7 0.7 copy-start.6
  124.4 0.8 copy-start.2

commit v3 on v2

--- a/solution.py
+++ b/solution.py
@@ -10,7 +10,8 @@
 AXES = ("win", "head")
 HEAD_DIM = 128
 PEERS = 8
-SIDE = (0, 1, 4, 5)
+ORDER = (4, 1, 2, 5, 6, 3, 7, 0)
+SIDE = (4, 1, 5, 0)
 
 
 def flat(band, core, x, z_lo):
@@ -78,7 +79,7 @@
     return pl.ds(start if isinstance(h, int) else pl.multiple_of(start, HEAD_DIM), HEAD_DIM)
 
 
-def split_even_kernel(east_ref, tokens_ref, out_ref):
+def split_even_kernel(where_ref, tokens_ref, out_ref):
     for h in range(PEERS):
         out_ref[h] = tokens_ref[..., lanes(h)]
 
@@ -88,41 +89,25 @@
         out_ref[...] = tokens_ref[..., lanes(where_ref[1] ^ k)]
 
 
-def split_even(tokens, east):
+def cut(kernel, name, where, tokens, odd, out_shape):
     kinds, rows, cols, channels = tokens.shape
-    half = cols // 2
+    vmem = pl.BlockSpec(memory_space=pltpu.VMEM)
     return pl.pallas_call(
-        split_even_kernel,
-        out_shape=jax.ShapeDtypeStruct((PEERS, kinds, rows, half, HEAD_DIM), tokens.dtype),
+        kernel,
+        out_shape=out_shape,
         grid_spec=pltpu.PrefetchScalarGridSpec(
             num_scalar_prefetch=1,
-            grid=(kinds,),
-            in_specs=[pl.BlockSpec((1, rows, half, channels), lambda t, east: (t, 0, east[0], 0))],
-            out_specs=pl.BlockSpec(
-                (PEERS, 1, rows, half, HEAD_DIM), lambda t, east: (0, t, 0, 0, 0)
-            ),
+            grid=(1,),
+            in_specs=[
+                pl.BlockSpec(
+                    (kinds, rows, cols // 2, channels),
+                    lambda t, where: (0, 0, where[0] if odd else 1 - where[0], 0),
+                )
+            ],
+            out_specs=jax.tree.map(lambda _: vmem, out_shape),
         ),
-        name="split_even",
-    )(east, tokens)
-
-
-def split_odd(tokens, where):
-    kinds, rows, cols, channels = tokens.shape
-    half = cols // 2
-    block = jax.ShapeDtypeStruct((kinds, rows, half, HEAD_DIM), tokens.dtype)
-    return pl.pallas_call(
-        split_odd_kernel,
-        out_shape=[block] * PEERS,
-        grid_spec=pltpu.PrefetchScalarGridSpec(
-            num_scalar_prefetch=1,
-            grid=(kinds,),
-            in_specs=[
-                pl.BlockSpec((1, rows, half, channels), lambda t, where: (t, 0, where[0], 0))
-            ],
-            out_specs=[pl.BlockSpec((1, rows, half, HEAD_DIM), lambda t, where: (t, 0, 0, 0))]
-            * PEERS,
-        ),
-        name="split_odd",
+        compiler_params=pltpu.CompilerParams(vmem_limit_bytes=32 * 2**20),
+        name=name,
     )(where, tokens)
 
 
@@ -163,10 +148,11 @@
 
 def attend_blocks(split_ref, blocks, outs, keys, values):
     count, width = blocks[0].shape[1:]
-    scale = 1.0 / math.sqrt(width)
+    scale = math.log2(math.e) / math.sqrt(width)
     for b, block in enumerate(blocks):
         keys[b * count : (b + 1) * count] = block[1]
-        values[b * count : (b + 1) * count] = block[2]
+        values[b * count : (b + 1) * count, :width] = block[2]
+    values[:, width:] = jnp.ones((values.shape[0], values.shape[1] - width), values.dtype)
     half = len(blocks) // 2
 
     def attend_one(b, low, high):
@@ -176,14 +162,12 @@
             (((1,), (1,)), ((), ())),
             preferred_element_type=jnp.float32,
         )
-        scores = scores * scale
         row_max = jnp.max(scores, axis=-1, keepdims=True)
-        weights = jnp.exp(scores - row_max)
-        row_total = jnp.sum(weights, axis=-1, keepdims=True)
+        weights = jnp.exp2(scores * scale - row_max * scale)
         mixture = jnp.dot(
             weights.astype(jnp.bfloat16), values[low:high], preferred_element_type=jnp.float32
         )
-        outs[b][...] = (mixture / row_total).astype(outs[b].dtype)
+        outs[b][...] = (mixture[:, :width] / mixture[:, width:]).astype(outs[b].dtype)
 
     @pl.when(split_ref[0] == 0)
     def _():
@@ -208,8 +192,10 @@
 
 
 def attend_odd_kernel(split_ref, *refs):
-    blocks, (own_ref, other_ref, keys, values) = refs[:PEERS], refs[PEERS:]
-    outs = [None] * PEERS
+    arrived, (own_ref, other_ref, keys, values) = refs[:PEERS], refs[PEERS:]
+    blocks, outs = [None] * PEERS, [None] * PEERS
+    for k, block in zip(ORDER, arrived):
+        blocks[k] = block
     for i, d in enumerate(SIDE):
         outs[d], outs[d ^ 2] = own_ref.at[i], other_ref.at[i]
     attend_blocks(split_ref, blocks, outs, keys, values)
@@ -223,7 +209,10 @@
         out_shape=out_shape,
         in_specs=[pl.BlockSpec(memory_space=pltpu.SMEM)] + [vmem] * len(operands),
         out_specs=jax.tree.map(lambda _: vmem, out_shape),
-        scratch_shapes=[pltpu.VMEM((PEERS * count, width), operands[0].dtype)] * 2,
+        scratch_shapes=[
+            pltpu.VMEM((PEERS * count, width), operands[0].dtype),
+            pltpu.VMEM((PEERS * count, 2 * width), operands[0].dtype),
+        ],
         compiler_params=pltpu.CompilerParams(vmem_limit_bytes=48 * 2**20),
         name=name,
     )(split, *operands)
@@ -237,22 +226,26 @@
     core, band_odd, x, z_lo = win & 1, (win >> 1) & 1, head >> 1, head & 1
     late = ((x == 2) | (x == 0)).astype(jnp.int32)
     member = late * 4 + (1 - band_odd) * 2 + z_lo
+    split = (((x == 3) & (core == 1)) | ((x == 0) & (core == 0))).astype(jnp.int32)
     where = jnp.stack([band_odd, member])
-    east = (1 - band_odd)[None]
-    split = (((x == 3) & (core == 1)) | ((x == 0) & (core == 0))).astype(jnp.int32)[None]
-
-    even = exchange(split_even(tokens, east), 0)
-    odd = split_odd(tokens, where)
-    odd = [lax.ppermute(odd[k], AXES, to_workers(1, k)) for k in range(PEERS)]
-
-    result = attend(
+    split = split[None]
+    block = jax.ShapeDtypeStruct((3, rows, half, HEAD_DIM), qkv.dtype)
+
+    even = jax.ShapeDtypeStruct((PEERS,) + block.shape, qkv.dtype)
+    even = cut(split_even_kernel, "split_even", where, tokens, False, even)
+    even = exchange(even, 0)
+    odd = cut(split_odd_kernel, "split_odd", where, tokens, True, [block] * PEERS)
+    odd = [lax.ppermute(odd[k], AXES, to_workers(1, k)) for k in ORDER]
+
+    even = attend(
         attend_even_kernel,
         "attend_even",
         split,
         [even.reshape(PEERS, 3, count, HEAD_DIM)],
         jax.ShapeDtypeStruct((PEERS, count, HEAD_DIM), qkv.dtype),
     )
-    even = exchange(result.reshape(PEERS, rows, half, HEAD_DIM), 0)
+    even, odd = lax.optimization_barrier((even, odd))
+    even = exchange(even.reshape(PEERS, rows, half, HEAD_DIM), 0)
 
     own, other = attend(
         attend_odd_kernel,

time: 129 us -> 120 us (0.930)
  waiting for transfers between devices: 15.9 us -> 5.29 us
  starting transfers between devices: 78 us -> 85.3 us
  Pallas kernels: 30.4 us -> 23.6 us
  local copies, waits for them, and re-layouts: 3.14 us -> 4.76 us
    ppermute x8, waiting for transfers between devices: 8.04 us -> 0.02 us  [body(): odd = [lax.ppermute(odd[k], AXES, to_workers(1, k)) for k in ORDER]]
    pallas_call x2, Pallas kernels: 7.99 us -> 2.88 us  [cut(): pl.pallas_call(kernel, out_shape=out_shape, grid_spec=pltpu.PrefetchScala...]
    ppermute x4, starting transfers between devices: 9.66 us -> 14.5 us  [body(): odd.append(lax.ppermute(pair, AXES, to_holders(1, d)))]
    ppermute x4, waiting for transfers between devices: 7.83 us -> 5.26 us  [body(): odd.append(lax.ppermute(pair, AXES, to_holders(1, d)))]
    ppermute x1, starting transfers between devices: 6.09 us -> 8.65 us  [body(): other = lax.ppermute(other, AXES, between_workers(1, 2))]
    all_to_all x2, starting transfers between devices: 16.7 us -> 14.3 us  [exchange(): lax.all_to_all(blocks, AXES, split_axis=0, concat_axis=0, axis_index_grou...]
    ppermute x8, starting transfers between devices: 45.5 us -> 47.8 us  [body(): odd = [lax.ppermute(odd[k], AXES, to_workers(1, k)) for k in ORDER]]
    pallas_call x2, Pallas kernels: 19.3 us -> 17.5 us  [attend(): pl.pallas_call(kernel, out_shape=out_shape, in_specs=[pl.BlockSpec(memory...]
  transfers between devices with their start and end apart: 15 -> 15, of which waited for: 4 -> 2; matrix products, arithmetic and copies ran while one was open for 1% -> 0% of each run, Pallas kernels for 18% -> 10%
where the time goes in v3:
time: 120 us; the launch traced here: 119 us
  starting transfers between devices  85.3 us (71%)
  Pallas kernels  23.6 us (20%)
  waiting for transfers between devices  5.29 us (4%)
  local copies, waits for them, and re-layouts  4.76 us (4%)
    ppermute x8, starting transfers between devices, body(): odd = [lax.ppermute(odd[k], AXES, to_workers(1, k)) for k in ORDER]  47.8 us
    pallas_call x2, Pallas kernels, attend(): pl.pallas_call(kernel, out_shape=out_shape, in_specs=[pl.BlockSpec(memory...  17.5 us
    ppermute x4, starting transfers between devices, body(): odd.append(lax.ppermute(pair, AXES, to_holders(1, d)))  14.5 us
    all_to_all x2, starting transfers between devices, exchange(): lax.all_to_all(blocks, AXES, split_axis=0, concat_axis=0, axis_index_grou...  14.3 us
    ppermute x1, starting transfers between devices, body(): other = lax.ppermute(other, AXES, between_workers(1, 2))  8.65 us
    ppermute x4, waiting for transfers between devices, body(): odd.append(lax.ppermute(pair, AXES, to_holders(1, d)))  5.26 us
    unnamed x18, local copies, waits for them, and re-layouts  4.72 us
    pallas_call x1, Pallas kernels, join_heads(): pl.pallas_call(join_kernel, out_shape=jax.ShapeDtypeStruct((rows, 2 * hal...  3.15 us
  transfers between devices with their start and end apart: 15, of which 2 were waited for; matrix products, arithmetic and copies ran while one was open for 0% of the time, Pallas kernels for 10%

profile of v3, /device:TPU:1, one launch (start us, length us, event | category | flops | bytes accessed | tf_op | source)
XLA Modules:
  0.0 119.4 jit_solution(17252805450206358095)
XLA Ops:
  0.0 0.1 pad_add_fusion.where_ref
  0.1 0.0 copy-start
  0.1 2.0 %copy-done = bf16[3,1,12,48,1024]{4,3,2,1,0:T(8,128)(2,1)S(1)} copy-done((bf16[3,1,12,48,1024]{4,3,2,1,0:T(8,128)(2,1)S(1)}, bf16[3,1,12,48,1024]{4,3,2,1,0:T(8,128)(2,1)}, u32[]{:S(2)}) %copy-start) | copy-done | bytes 3538968
  2.1 1.0 split_even.1
  3.1 0.0 copy-start.2
  3.1 1.2 copy-done.2
  4.3 8.8 %all-to-all-start = ((bf16[8,3,12,24,128]{4,3,2,1,0:T(8,128)(2,1)}), bf16[8,3,12,24,128]{4,3,2,1,0:T(8,128)(2,1)}, u32[]{:S(2)}, u32[]{:S(2)}) async-start(bf16[8,3,12,24,128]{4,3,2,1,0:T(8,128)(2,1)} %copy-done.2), calls=%async_computation | async-start | bytes 3538944 | tf_op jit(solution)/shard_map/all_to_all | solution.py:67
  13.1 0.0 copy-done.3
  13.1 0.0 copy-done.1
  13.1 1.9 %split_odd.1 = (bf16[3,12,24,128]{3,2,1,0:T(8,128)(2,1)}, bf16[3,12,24,128]{3,2,1,0:T(8,128)(2,1)S(1)}, bf16[3,12,24,128]{3,2,1,0:T(8,128)(2,1)S(1)}, bf16[3,12,...) custom-call(s32[2]{0:T(128)S(1)} %pad_add_fusion.where_ref, ...), custom_call_target="tpu_custom_call" | custom-call | tf_op jit(solution)/shard_map/split_odd/pallas_call | solution.py:95
  15.0 1.9 %collective-permute-start = (bf16[3,12,24,128]{3,2,1,0:T(8,128)(2,1)S(1)}, bf16[3,12,24,128]{3,2,1,0:T(8,128)(2,1)S(1)}, u32[]{:S(2)}, u32[]{:S(2)}) collective-permute-start(bf16[3,12,24,128]{3,2,1,0:T(8,128)(2,1)S(1)} %get-tuple-element.24), channel_id=1, source_target_pairs={{18,20},{19,21},{34,36},{35,37},{20,18},{21,19},{36,34},{37,35},{2... | collective-permute-start | bytes 663560 | tf_op jit(solution)/shard_map/ppermute | solution.py:238
  16.9 10.7 %collective-permute-start.1 = (bf16[3,12,24,128]{3,2,1,0:T(8,128)(2,1)S(1)}, bf16[3,12,24,128]{3,2,1,0:T(8,128)(2,1)S(1)}, u32[]{:S(2)}, u32[]{:S(2)}) collective-permute-start(bf16[3,12,24,128]{3,2,1,0:T(8,128)(2,1)S(1)} %get-tuple-element.25), channel_id=1, source_target_pairs={{18,19},{19,18},{34,35},{35,34},{20,21},{21,20},{36,37},{37,36},{2... | collective-permute-start | bytes 663560 | tf_op jit(solution)/shard_map/ppermute | solution.py:238
  27.6 1.9 %collective-permute-start.2 = (bf16[3,12,24,128]{3,2,1,0:T(8,128)(2,1)S(1)}, bf16[3,12,24,128]{3,2,1,0:T(8,128)(2,1)S(1)}, u32[]{:S(2)}, u32[]{:S(2)}) collective-permute-start(bf16[3,12,24,128]{3,2,1,0:T(8,128)(2,1)S(1)} %get-tuple-element.26), channel_id=1, source_target_pairs={{18,34},{19,35},{34,18},{35,19},{20,36},{21,37},{36,20},{37,21},{2... | collective-permute-start | bytes 663560 | tf_op jit(solution)/shard_map/ppermute | solution.py:238
  29.5 8.3 %collective-permute-start.3 = (bf16[3,12,24,128]{3,2,1,0:T(8,128)(2,1)}, bf16[3,12,24,128]{3,2,1,0:T(8,128)(2,1)S(1)}, u32[]{:S(2)}, u32[]{:S(2)}) collective-permute-start(bf16[3,12,24,128]{3,2,1,0:T(8,128)(2,1)} %get-tuple-element.27), channel_id=1, source_target_pairs={{18,21},{19,20},{34,37},{35,36},{20,19},{21,18},{36,35},{37,34},{2... | collective-permute-start | bytes 663560 | tf_op jit(solution)/shard_map/ppermute | solution.py:238
  37.9 2.7 %collective-permute-start.4 = (bf16[3,12,24,128]{3,2,1,0:T(8,128)(2,1)}, bf16[3,12,24,128]{3,2,1,0:T(8,128)(2,1)S(1)}, u32[]{:S(2)}, u32[]{:S(2)}) collective-permute-start(bf16[3,12,24,128]{3,2,1,0:T(8,128)(2,1)} %get-tuple-element.28), channel_id=1, source_target_pairs={{18,36},{19,37},{34,20},{35,21},{20,34},{21,35},{36,18},{37,19},{2... | collective-permute-start | bytes 663560 | tf_op jit(solution)/shard_map/ppermute | solution.py:238
  40.6 0.0 collective-permute-done
  40.6 11.3 %collective-permute-start.5 = (bf16[3,12,24,128]{3,2,1,0:T(8,128)(2,1)}, bf16[3,12,24,128]{3,2,1,0:T(8,128)(2,1)S(1)}, u32[]{:S(2)}, u32[]{:S(2)}) collective-permute-start(bf16[3,12,24,128]{3,2,1,0:T(8,128)(2,1)} %get-tuple-element.29), channel_id=1, source_target_pairs={{18,35},{19,34},{34,19},{35,18},{20,37},{21,36},{36,21},{37,20},{2... | collective-permute-start | bytes 663560 | tf_op jit(solution)/shard_map/ppermute | solution.py:238
  51.9 0.0 collective-permute-done.1
  51.9 9.4 %collective-permute-start.6 = (bf16[3,12,24,128]{3,2,1,0:T(8,128)(2,1)}, bf16[3,12,24,128]{3,2,1,0:T(8,128)(2,1)S(1)}, u32[]{:S(2)}, u32[]{:S(2)}) collective-permute-start(bf16[3,12,24,128]{3,2,1,0:T(8,128)(2,1)} %get-tuple-element.30), channel_id=1, source_target_pairs={{18,37},{19,36},{34,21},{35,20},{20,35},{21,34},{36,19},{37,18},{2... | collective-permute-start | bytes 663560 | tf_op jit(solution)/shard_map/ppermute | solution.py:238
  61.3 0.0 collective-permute-done.2
  61.3 1.6 %collective-permute-start.7 = (bf16[3,12,24,128]{3,2,1,0:T(8,128)(2,1)}, bf16[3,12,24,128]{3,2,1,0:T(8,128)(2,1)S(1)}, u32[]{:S(2)}, u32[]{:S(2)}) collective-permute-start(bf16[3,12,24,128]{3,2,1,0:T(8,128)(2,1)} %get-tuple-element.31), channel_id=1, source_target_pairs={{18,18},{19,19},{34,34},{35,35},{20,20},{21,21},{36,36},{37,37},{2... | collective-permute-start | bytes 663560 | tf_op jit(solution)/shard_map/ppermute | solution.py:238
  62.9 0.0 all-to-all-done
  62.9 9.9 %attend_even.1 = bf16[8,288,128]{2,1,0:T(8,128)(2,1)} custom-call(s32[1]{0:T(128)} %bitcast.2.split_ref, bf16[8,3,288,128]{3,2,1,0:T(8,128)(2,1)} %bitcast.4.qkv_ref), custom_call_target="tpu_custom_call" | custom-call | tf_op jit(solution)/shard_map/attend_even/pallas_call | solution.py:207
  72.7 0.0 collective-permute-done.3
  72.7 0.0 collective-permute-done.4
  72.7 0.0 collective-permute-done.5
  72.7 0.0 collective-permute-done.6
  72.8 0.0 collective-permute-done.7
  72.8 7.7 %attend_odd.1 = (bf16[4,288,128]{2,1,0:T(8,128)(2,1)S(1)}, bf16[4,288,128]{2,1,0:T(8,128)(2,1)S(1)}) custom-call(s32[1]{0:T(128)} %bitcast.2.split_ref, bf16[3,288,128]{2,1,0:T(8,128)(2,1)S(1)} %bitcast.21, bf16[3,288,128]{2,1,0:T(8,128)(2,1)S(1)} %bitcast.22, bf16[3,288,128]{2,1,0:T(8,128)(2,1)S(1)} %bitcast.23, bf16[3,288,128]{2,1,0:T(8,128)(2,1)S(1)} %bitcast.24, ...), custom_call_target="tpu_custom_call" | custom-call | tf_op jit(solution)/shard_map/attend_odd/pallas_call | solution.py:207
  80.5 8.7 %collective-permute-start.8 = (bf16[4,288,128]{2,1,0:T(8,128)(2,1)S(1)}, bf16[4,288,128]{2,1,0:T(8,128)(2,1)S(1)}, u32[]{:S(2)}, u32[]{:S(2)}) collective-permute-start(bf16[4,288,128]{2,1,0:T(8,128)(2,1)S(1)} %get-tuple-element.42), channel_id=1, source_target_pairs={{18,34},{19,35},{34,18},{35,19},{20,36},{21,37},{36,20},{37,21},{2... | collective-permute-start | bytes 884744 | tf_op jit(solution)/shard_map/ppermute | solution.py:257
  89.1 5.5 %all-to-all-start.1 = ((bf16[8,12,24,128]{3,2,1,0:T(8,128)(2,1)}), bf16[8,12,24,128]{3,2,1,0:T(8,128)(2,1)S(1)}, u32[]{:S(2)}, u32[]{:S(2)}) async-start(bf16[8,12,24,128]{3,2,1,0:T(8,128)(2,1)} %bitcast.5), calls=%async_computation.1 | async-start | bytes 1179648 | tf_op jit(solution)/shard_map/all_to_all | solution.py:67
  94.7 0.0 collective-permute-done.8
  94.7 1.9 %collective-permute-start.9 = (bf16[2,12,24,128]{3,2,1,0:T(8,128)(2,1)S(1)}, bf16[2,12,24,128]{3,2,1,0:T(8,128)(2,1)S(1)}, u32[]{:S(2)}, u32[]{:S(2)}) collective-permute-start(bf16[2,12,24,128]{3,2,1,0:T(8,128)(2,1)S(1)} %bitcast.29), channel_id=1, source_target_pairs={{20,18},{21,19},{36,34},{37,35},{18,20},{19,21},{34,36},{35,37},{2... | collective-permute-start | bytes 442376 | tf_op jit(solution)/shard_map/ppermute | solution.py:261
  96.7 7.9 %collective-permute-start.10 = (bf16[2,12,24,128]{3,2,1,0:T(8,128)(2,1)S(1)}, bf16[2,12,24,128]{3,2,1,0:T(8,128)(2,1)S(1)}, u32[]{:S(2)}, u32[]{:S(2)}) collective-permute-start(bf16[2,12,24,128]{3,2,1,0:T(8,128)(2,1)S(1)} %bitcast.30), channel_id=1, source_target_pairs={{19,18},{18,19},{35,34},{34,35},{21,20},{20,21},{37,36},{36,37},{2... | collective-permute-start | bytes 442376 | tf_op jit(solution)/shard_map/ppermute | solution.py:261
  104.6 4.0 %collective-permute-start.11 = (bf16[2,12,24,128]{3,2,1,0:T(8,128)(2,1)S(1)}, bf16[2,12,24,128]{3,2,1,0:T(8,128)(2,1)S(1)}, u32[]{:S(2)}, u32[]{:S(2)}) collective-permute-start(bf16[2,12,24,128]{3,2,1,0:T(8,128)(2,1)S(1)} %bitcast.31), channel_id=1, source_target_pairs={{21,18},{20,19},{37,34},{36,35},{19,20},{18,21},{35,36},{34,37},{2... | collective-permute-start | bytes 442376 | tf_op jit(solution)/shard_map/ppermute | solution.py:261
  108.7 0.7 collective-permute-start.12
  109.4 0.0 collective-permute-done.9.refs_0_
  109.4 0.0 copy-start.5
  109.4 0.1 collective-permute-done.10.refs_1_
  109.5 5.1 %collective-permute-done.11.refs_2_ = bf16[2,12,24,128]{3,2,1,0:T(8,128)(2,1)S(1)} collective-permute-done((bf16[2,12,24,128]{3,2,1,0:T(8,128)(2,1)S(1)}, bf16[2,12,24,128]{3,2,1,0:T(8,128)(2,1)S(1)}, u32[]{:S(2)}, u32[]{:S(2)}) %collective-permute-start.11) | collective-permute-done | bytes 147488 | tf_op jit(solution)/shard_map/ppermute | solution.py:261
  114.7 0.0 collective-permute-done.12.refs_3_
  114.7 0.0 all-to-all-done.1.even_ref
  114.7 0.0 copy-done.5
  114.7 0.0 copy-done.6
  114.7 0.6 copy-done.7
  115.3 0.0 copy-done.8
  115.4 0.8 copy-done.4
  116.2 3.2 %join_heads.1 = bf16[12,48,1024]{2,1,0:T(8,128)(2,1)} custom-call(s32[2]{0:T(128)} %copy-done.3, bf16[8,12,24,128]{3,2,1,0:T(8,128)(2,1)} %copy-done.4, bf16[2,12,24,128]{3,2,1,0:T(8,128)(2,1)} %copy-done.5, bf16[2,12,24,128]{3,2,1,0:T(8,128)(2,1)} %copy-done.6, bf16[2,12,24,128]{3,2,1,0:T(8,128)(2,1)} %copy-done.7, bf16[2,12,24,128]{3,2,1,0:T(8,128)(2,1)} %copy-done.8), custom_call_target="tpu_custom_call" | custom-call | tf_op jit(solution)/shard_map/join_heads/pallas_call | solution.py:136
  (12 shorter events, 0.1 us)
Async XLA Ops:
  0.1 13.0 %copy-start.3 = (s32[2]{0:T(128)}, s32[2]{0:T(128)S(1)}, u32[]{:S(2)}) copy-start(s32[2]{0:T(128)S(1)} %pad_add_fusion.where_ref) | copy-start | bytes 28
  0.1 2.0 %copy-start = (bf16[3,1,12,48,1024]{4,3,2,1,0:T(8,128)(2,1)S(1)}, bf16[3,1,12,48,1024]{4,3,2,1,0:T(8,128)(2,1)}, u32[]{:S(2)}) copy-start(bf16[3,1,12,48,1024]{4,3,2,1,0:T(8,128)(2,1)} %param.1) | copy-start | bytes 10616836
  3.1 1.2 copy-start.2
  4.3 8.8 %copy-start.1 = (bf16[3,1,12,48,1024]{4,3,2,1,0:T(8,128)(2,1)S(1)}, bf16[3,1,12,48,1024]{4,3,2,1,0:T(8,128)(2,1)}, u32[]{:S(2)}) copy-start(bf16[3,1,12,48,1024]{4,3,2,1,0:T(8,128)(2,1)} %param.1) | copy-start | bytes 10616836
  4.3 58.6 %all-to-all-start = ((bf16[8,3,12,24,128]{4,3,2,1,0:T(8,128)(2,1)}), bf16[8,3,12,24,128]{4,3,2,1,0:T(8,128)(2,1)}, u32[]{:S(2)}, u32[]{:S(2)}) async-start(bf16[8,3,12,24,128]{4,3,2,1,0:T(8,128)(2,1)} %copy-done.2), calls=%async_computation | async-start | bytes 3538944 | tf_op jit(solution)/shard_map/all_to_all | solution.py:67
  15.0 25.6 %collective-permute-start = (bf16[3,12,24,128]{3,2,1,0:T(8,128)(2,1)S(1)}, bf16[3,12,24,128]{3,2,1,0:T(8,128)(2,1)S(1)}, u32[]{:S(2)}, u32[]{:S(2)}) collective-permute-start(bf16[3,12,24,128]{3,2,1,0:T(8,128)(2,1)S(1)} %get-tuple-element.24), channel_id=1, source_target_pairs={{18,20},{19,21},{34,36},{35,37},{20,18},{21,19},{36,34},{37,35},{2... | collective-permute-start | bytes 663560 | tf_op jit(solution)/shard_map/ppermute | solution.py:238
  16.9 35.0 %collective-permute-start.1 = (bf16[3,12,24,128]{3,2,1,0:T(8,128)(2,1)S(1)}, bf16[3,12,24,128]{3,2,1,0:T(8,128)(2,1)S(1)}, u32[]{:S(2)}, u32[]{:S(2)}) collective-permute-start(bf16[3,12,24,128]{3,2,1,0:T(8,128)(2,1)S(1)} %get-tuple-element.25), channel_id=1, source_target_pairs={{18,19},{19,18},{34,35},{35,34},{20,21},{21,20},{36,37},{37,36},{2... | collective-permute-start | bytes 663560 | tf_op jit(solution)/shard_map/ppermute | solution.py:238
  27.6 33.7 %collective-permute-start.2 = (bf16[3,12,24,128]{3,2,1,0:T(8,128)(2,1)S(1)}, bf16[3,12,24,128]{3,2,1,0:T(8,128)(2,1)S(1)}, u32[]{:S(2)}, u32[]{:S(2)}) collective-permute-start(bf16[3,12,24,128]{3,2,1,0:T(8,128)(2,1)S(1)} %get-tuple-element.26), channel_id=1, source_target_pairs={{18,34},{19,35},{34,18},{35,19},{20,36},{21,37},{36,20},{37,21},{2... | collective-permute-start | bytes 663560 | tf_op jit(solution)/shard_map/ppermute | solution.py:238
  29.5 43.2 %collective-permute-start.3 = (bf16[3,12,24,128]{3,2,1,0:T(8,128)(2,1)}, bf16[3,12,24,128]{3,2,1,0:T(8,128)(2,1)S(1)}, u32[]{:S(2)}, u32[]{:S(2)}) collective-permute-start(bf16[3,12,24,128]{3,2,1,0:T(8,128)(2,1)} %get-tuple-element.27), channel_id=1, source_target_pairs={{18,21},{19,20},{34,37},{35,36},{20,19},{21,18},{36,35},{37,34},{2... | collective-permute-start | bytes 663560 | tf_op jit(solution)/shard_map/ppermute | solution.py:238
  37.9 34.9 %collective-permute-start.4 = (bf16[3,12,24,128]{3,2,1,0:T(8,128)(2,1)}, bf16[3,12,24,128]{3,2,1,0:T(8,128)(2,1)S(1)}, u32[]{:S(2)}, u32[]{:S(2)}) collective-permute-start(bf16[3,12,24,128]{3,2,1,0:T(8,128)(2,1)} %get-tuple-element.28), channel_id=1, source_target_pairs={{18,36},{19,37},{34,20},{35,21},{20,34},{21,35},{36,18},{37,19},{2... | collective-permute-start | bytes 663560 | tf_op jit(solution)/shard_map/ppermute | solution.py:238
  40.6 32.2 %collective-permute-start.5 = (bf16[3,12,24,128]{3,2,1,0:T(8,128)(2,1)}, bf16[3,12,24,128]{3,2,1,0:T(8,128)(2,1)S(1)}, u32[]{:S(2)}, u32[]{:S(2)}) collective-permute-start(bf16[3,12,24,128]{3,2,1,0:T(8,128)(2,1)} %get-tuple-element.29), channel_id=1, source_target_pairs={{18,35},{19,34},{34,19},{35,18},{20,37},{21,36},{36,21},{37,20},{2... | collective-permute-start | bytes 663560 | tf_op jit(solution)/shard_map/ppermute | solution.py:238
  51.9 20.9 %collective-permute-start.6 = (bf16[3,12,24,128]{3,2,1,0:T(8,128)(2,1)}, bf16[3,12,24,128]{3,2,1,0:T(8,128)(2,1)S(1)}, u32[]{:S(2)}, u32[]{:S(2)}) collective-permute-start(bf16[3,12,24,128]{3,2,1,0:T(8,128)(2,1)} %get-tuple-element.30), channel_id=1, source_target_pairs={{18,37},{19,36},{34,21},{35,20},{20,35},{21,34},{36,19},{37,18},{2... | collective-permute-start | bytes 663560 | tf_op jit(solution)/shard_map/ppermute | solution.py:238
  61.3 11.5 %collective-permute-start.7 = (bf16[3,12,24,128]{3,2,1,0:T(8,128)(2,1)}, bf16[3,12,24,128]{3,2,1,0:T(8,128)(2,1)S(1)}, u32[]{:S(2)}, u32[]{:S(2)}) collective-permute-start(bf16[3,12,24,128]{3,2,1,0:T(8,128)(2,1)} %get-tuple-element.31), channel_id=1, source_target_pairs={{18,18},{19,19},{34,34},{35,35},{20,20},{21,21},{36,36},{37,37},{2... | collective-permute-start | bytes 663560 | tf_op jit(solution)/shard_map/ppermute | solution.py:238
  80.5 14.2 %collective-permute-start.8 = (bf16[4,288,128]{2,1,0:T(8,128)(2,1)S(1)}, bf16[4,288,128]{2,1,0:T(8,128)(2,1)S(1)}, u32[]{:S(2)}, u32[]{:S(2)}) collective-permute-start(bf16[4,288,128]{2,1,0:T(8,128)(2,1)S(1)} %get-tuple-element.42), channel_id=1, source_target_pairs={{18,34},{19,35},{34,18},{35,19},{20,36},{21,37},{36,20},{37,21},{2... | collective-permute-start | bytes 884744 | tf_op jit(solution)/shard_map/ppermute | solution.py:257
  89.1 25.5 %all-to-all-start.1 = ((bf16[8,12,24,128]{3,2,1,0:T(8,128)(2,1)}), bf16[8,12,24,128]{3,2,1,0:T(8,128)(2,1)S(1)}, u32[]{:S(2)}, u32[]{:S(2)}) async-start(bf16[8,12,24,128]{3,2,1,0:T(8,128)(2,1)} %bitcast.5), calls=%async_computation.1 | async-start | bytes 1179648 | tf_op jit(solution)/shard_map/all_to_all | solution.py:67
  94.7 14.7 %collective-permute-start.9 = (bf16[2,12,24,128]{3,2,1,0:T(8,128)(2,1)S(1)}, bf16[2,12,24,128]{3,2,1,0:T(8,128)(2,1)S(1)}, u32[]{:S(2)}, u32[]{:S(2)}) collective-permute-start(bf16[2,12,24,128]{3,2,1,0:T(8,128)(2,1)S(1)} %bitcast.29), channel_id=1, source_target_pairs={{20,18},{21,19},{36,34},{37,35},{18,20},{19,21},{34,36},{35,37},{2... | collective-permute-start | bytes 442376 | tf_op jit(solution)/shard_map/ppermute | solution.py:261
  96.7 12.8 %collective-permute-start.10 = (bf16[2,12,24,128]{3,2,1,0:T(8,128)(2,1)S(1)}, bf16[2,12,24,128]{3,2,1,0:T(8,128)(2,1)S(1)}, u32[]{:S(2)}, u32[]{:S(2)}) collective-permute-start(bf16[2,12,24,128]{3,2,1,0:T(8,128)(2,1)S(1)} %bitcast.30), channel_id=1, source_target_pairs={{19,18},{18,19},{35,34},{34,35},{21,20},{20,21},{37,36},{36,37},{2... | collective-permute-start | bytes 442376 | tf_op jit(solution)/shard_map/ppermute | solution.py:261
  104.6 10.0 %collective-permute-start.11 = (bf16[2,12,24,128]{3,2,1,0:T(8,128)(2,1)S(1)}, bf16[2,12,24,128]{3,2,1,0:T(8,128)(2,1)S(1)}, u32[]{:S(2)}, u32[]{:S(2)}) collective-permute-start(bf16[2,12,24,128]{3,2,1,0:T(8,128)(2,1)S(1)} %bitcast.31), channel_id=1, source_target_pairs={{21,18},{20,19},{37,34},{36,35},{19,20},{18,21},{35,36},{34,37},{2... | collective-permute-start | bytes 442376 | tf_op jit(solution)/shard_map/ppermute | solution.py:261
  108.7 6.0 %collective-permute-start.12 = (bf16[2,12,24,128]{3,2,1,0:T(8,128)(2,1)S(1)}, bf16[2,12,24,128]{3,2,1,0:T(8,128)(2,1)S(1)}, u32[]{:S(2)}, u32[]{:S(2)}) collective-permute-start(bf16[2,12,24,128]{3,2,1,0:T(8,128)(2,1)S(1)} %bitcast.32), channel_id=1, source_target_pairs={{18,18},{19,19},{34,34},{35,35},{20,20},{21,21},{36,36},{37,37},{2... | collective-permute-start | bytes 442376 | tf_op jit(solution)/shard_map/ppermute | solution.py:261
  109.4 5.3 %copy-start.5 = (bf16[2,12,24,128]{3,2,1,0:T(8,128)(2,1)}, bf16[2,12,24,128]{3,2,1,0:T(8,128)(2,1)S(1)}, u32[]{:S(2)}) copy-start(bf16[2,12,24,128]{3,2,1,0:T(8,128)(2,1)S(1)} %collective-permute-done.9.refs_0_) | copy-start | bytes 442372
  109.5 5.2 %copy-start.6 = (bf16[2,12,24,128]{3,2,1,0:T(8,128)(2,1)}, bf16[2,12,24,128]{3,2,1,0:T(8,128)(2,1)S(1)}, u32[]{:S(2)}) copy-start(bf16[2,12,24,128]{3,2,1,0:T(8,128)(2,1)S(1)} %collective-permute-done.10.refs_1_) | copy-start | bytes 442372
  114.7 0.7 copy-start.7
  114.7 0.7 copy-start.8
  115.4 0.8 copy-start.4

commit v4 on v3

--- a/solution.py
+++ b/solution.py
@@ -10,7 +10,7 @@
 AXES = ("win", "head")
 HEAD_DIM = 128
 PEERS = 8
-ORDER = (4, 1, 2, 5, 6, 3, 7, 0)
+ORDER = (2, 1, 4, 3, 6, 5, 7, 0)
 SIDE = (4, 1, 5, 0)
 
 

time: 120 us -> 117 us (0.975)
  the two profiles are of different devices: /device:TPU:1 before, /device:TPU:65 now
where the time goes in v4:
time: 117 us
  starting transfers between devices  83.4 us (71%)
  Pallas kernels  23.6 us (20%)
  local copies, waits for them, and re-layouts  4.69 us (4%)
  waiting for transfers between devices  4.59 us (4%)
    ppermute x8, starting transfers between devices, body(): odd = [lax.ppermute(odd[k], AXES, to_workers(1, k)) for k in ORDER]  40.6 us
    all_to_all x2, starting transfers between devices, exchange(): lax.all_to_all(blocks, AXES, split_axis=0, concat_axis=0, axis_index_grou...  21.5 us
    ppermute x4, starting transfers between devices, body(): odd.append(lax.ppermute(pair, AXES, to_holders(1, d)))  18.8 us
    pallas_call x2, Pallas kernels, attend(): pl.pallas_call(kernel, out_shape=out_shape, in_specs=[pl.BlockSpec(memory...  17.5 us
    unnamed x18, local copies, waits for them, and re-layouts  4.65 us
    ppermute x4, waiting for transfers between devices, body(): odd.append(lax.ppermute(pair, AXES, to_holders(1, d)))  4.56 us
    pallas_call x1, Pallas kernels, join_heads(): pl.pallas_call(join_kernel, out_shape=jax.ShapeDtypeStruct((rows, 2 * hal...  3.16 us
    pallas_call x2, Pallas kernels, cut(): pl.pallas_call(kernel, out_shape=out_shape, grid_spec=pltpu.PrefetchScala...  2.88 us
  transfers between devices with their start and end apart: 15, of which 1 were waited for; matrix products, arithmetic and copies ran while one was open for 0% of the time, Pallas kernels for 10%

profile of v4, /device:TPU:65, one launch (start us, length us, event | category | flops | bytes accessed | tf_op | source)
XLA Modules:
  0.0 116.7 jit_solution(2556212781955908560)
XLA Ops:
  0.0 0.1 pad_add_fusion.where_ref
  0.1 2.0 %copy-done = bf16[3,1,12,48,1024]{4,3,2,1,0:T(8,128)(2,1)S(1)} copy-done((bf16[3,1,12,48,1024]{4,3,2,1,0:T(8,128)(2,1)S(1)}, bf16[3,1,12,48,1024]{4,3,2,1,0:T(8,128)(2,1)}, u32[]{:S(2)}) %copy-start) | copy-done | bytes 3538968
  2.1 1.0 split_even.1
  3.1 0.0 copy-start.2
  3.1 1.2 %copy-done.2 = bf16[8,3,12,24,128]{4,3,2,1,0:T(8,128)(2,1)} copy-done((bf16[8,3,12,24,128]{4,3,2,1,0:T(8,128)(2,1)}, bf16[8,3,12,24,128]{4,3,2,1,0:T(8,128)(2,1)S(1)}, u32[]{:S(2)}) %copy-start.2) | copy-done | bytes 1769496
  4.3 7.1 %all-to-all-start = ((bf16[8,3,12,24,128]{4,3,2,1,0:T(8,128)(2,1)}), bf16[8,3,12,24,128]{4,3,2,1,0:T(8,128)(2,1)}, u32[]{:S(2)}, u32[]{:S(2)}) async-start(bf16[8,3,12,24,128]{4,3,2,1,0:T(8,128)(2,1)} %copy-done.2), calls=%async_computation | async-start | bytes 3538944 | tf_op jit(solution)/shard_map/all_to_all | solution.py:67
  11.3 0.0 copy-done.3
  11.3 0.0 copy-done.1
  11.3 1.9 %split_odd.1 = (bf16[3,12,24,128]{3,2,1,0:T(8,128)(2,1)}, bf16[3,12,24,128]{3,2,1,0:T(8,128)(2,1)S(1)}, bf16[3,12,24,128]{3,2,1,0:T(8,128)(2,1)S(1)}, bf16[3,12,...) custom-call(s32[2]{0:T(128)S(1)} %pad_add_fusion.where_ref, ...), custom_call_target="tpu_custom_call" | custom-call | tf_op jit(solution)/shard_map/split_odd/pallas_call | solution.py:95
  13.2 13.9 %collective-permute-start = (bf16[3,12,24,128]{3,2,1,0:T(8,128)(2,1)S(1)}, bf16[3,12,24,128]{3,2,1,0:T(8,128)(2,1)S(1)}, u32[]{:S(2)}, u32[]{:S(2)}) collective-permute-start(bf16[3,12,24,128]{3,2,1,0:T(8,128)(2,1)S(1)} %get-tuple-element.24), channel_id=1, source_target_pairs={{18,34},{19,35},{34,18},{35,19},{20,36},{21,37},{36,20},{37,21},{2... | collective-permute-start | bytes 663560 | tf_op jit(solution)/shard_map/ppermute | solution.py:238
  27.1 1.9 %collective-permute-start.1 = (bf16[3,12,24,128]{3,2,1,0:T(8,128)(2,1)S(1)}, bf16[3,12,24,128]{3,2,1,0:T(8,128)(2,1)S(1)}, u32[]{:S(2)}, u32[]{:S(2)}) collective-permute-start(bf16[3,12,24,128]{3,2,1,0:T(8,128)(2,1)S(1)} %get-tuple-element.25), channel_id=1, source_target_pairs={{18,19},{19,18},{34,35},{35,34},{20,21},{21,20},{36,37},{37,36},{2... | collective-permute-start | bytes 663560 | tf_op jit(solution)/shard_map/ppermute | solution.py:238
  29.1 3.3 %collective-permute-start.2 = (bf16[3,12,24,128]{3,2,1,0:T(8,128)(2,1)S(1)}, bf16[3,12,24,128]{3,2,1,0:T(8,128)(2,1)S(1)}, u32[]{:S(2)}, u32[]{:S(2)}) collective-permute-start(bf16[3,12,24,128]{3,2,1,0:T(8,128)(2,1)S(1)} %get-tuple-element.26), channel_id=1, source_target_pairs={{18,20},{19,21},{34,36},{35,37},{20,18},{21,19},{36,34},{37,35},{2... | collective-permute-start | bytes 663560 | tf_op jit(solution)/shard_map/ppermute | solution.py:238
  32.3 1.9 %collective-permute-start.3 = (bf16[3,12,24,128]{3,2,1,0:T(8,128)(2,1)}, bf16[3,12,24,128]{3,2,1,0:T(8,128)(2,1)S(1)}, u32[]{:S(2)}, u32[]{:S(2)}) collective-permute-start(bf16[3,12,24,128]{3,2,1,0:T(8,128)(2,1)} %get-tuple-element.27), channel_id=1, source_target_pairs={{18,35},{19,34},{34,19},{35,18},{20,37},{21,36},{36,21},{37,20},{2... | collective-permute-start | bytes 663560 | tf_op jit(solution)/shard_map/ppermute | solution.py:238
  34.3 8.6 %collective-permute-start.4 = (bf16[3,12,24,128]{3,2,1,0:T(8,128)(2,1)}, bf16[3,12,24,128]{3,2,1,0:T(8,128)(2,1)S(1)}, u32[]{:S(2)}, u32[]{:S(2)}) collective-permute-start(bf16[3,12,24,128]{3,2,1,0:T(8,128)(2,1)} %get-tuple-element.28), channel_id=1, source_target_pairs={{18,36},{19,37},{34,20},{35,21},{20,34},{21,35},{36,18},{37,19},{2... | collective-permute-start | bytes 663560 | tf_op jit(solution)/shard_map/ppermute | solution.py:238
  42.9 0.0 collective-permute-done
  42.9 1.9 %collective-permute-start.5 = (bf16[3,12,24,128]{3,2,1,0:T(8,128)(2,1)}, bf16[3,12,24,128]{3,2,1,0:T(8,128)(2,1)S(1)}, u32[]{:S(2)}, u32[]{:S(2)}) collective-permute-start(bf16[3,12,24,128]{3,2,1,0:T(8,128)(2,1)} %get-tuple-element.29), channel_id=1, source_target_pairs={{18,21},{19,20},{34,37},{35,36},{20,19},{21,18},{36,35},{37,34},{2... | collective-permute-start | bytes 663560 | tf_op jit(solution)/shard_map/ppermute | solution.py:238
  44.8 0.0 collective-permute-done.1
  44.8 3.1 %collective-permute-start.6 = (bf16[3,12,24,128]{3,2,1,0:T(8,128)(2,1)}, bf16[3,12,24,128]{3,2,1,0:T(8,128)(2,1)S(1)}, u32[]{:S(2)}, u32[]{:S(2)}) collective-permute-start(bf16[3,12,24,128]{3,2,1,0:T(8,128)(2,1)} %get-tuple-element.30), channel_id=1, source_target_pairs={{18,37},{19,36},{34,21},{35,20},{20,35},{21,34},{36,19},{37,18},{2... | collective-permute-start | bytes 663560 | tf_op jit(solution)/shard_map/ppermute | solution.py:238
  47.9 0.0 collective-permute-done.2
  47.9 6.0 %collective-permute-start.7 = (bf16[3,12,24,128]{3,2,1,0:T(8,128)(2,1)}, bf16[3,12,24,128]{3,2,1,0:T(8,128)(2,1)S(1)}, u32[]{:S(2)}, u32[]{:S(2)}) collective-permute-start(bf16[3,12,24,128]{3,2,1,0:T(8,128)(2,1)} %get-tuple-element.31), channel_id=1, source_target_pairs={{18,18},{19,19},{34,34},{35,35},{20,20},{21,21},{36,36},{37,37},{2... | collective-permute-start | bytes 663560 | tf_op jit(solution)/shard_map/ppermute | solution.py:238
  53.9 0.0 all-to-all-done
  53.9 9.9 %attend_even.1 = bf16[8,288,128]{2,1,0:T(8,128)(2,1)} custom-call(s32[1]{0:T(128)} %bitcast.2.split_ref, bf16[8,3,288,128]{3,2,1,0:T(8,128)(2,1)} %bitcast.4.qkv_ref), custom_call_target="tpu_custom_call" | custom-call | tf_op jit(solution)/shard_map/attend_even/pallas_call | solution.py:207
  63.8 0.0 collective-permute-done.3
  63.8 0.0 collective-permute-done.4
  63.8 0.0 collective-permute-done.5
  63.8 0.0 collective-permute-done.6
  63.8 0.0 collective-permute-done.7
  63.8 7.7 %attend_odd.1 = (bf16[4,288,128]{2,1,0:T(8,128)(2,1)S(1)}, bf16[4,288,128]{2,1,0:T(8,128)(2,1)S(1)}) custom-call(s32[1]{0:T(128)} %bitcast.2.split_ref, bf16[3,288,128]{2,1,0:T(8,128)(2,1)S(1)} %bitcast.21, bf16[3,288,128]{2,1,0:T(8,128)(2,1)S(1)} %bitcast.22, bf16[3,288,128]{2,1,0:T(8,128)(2,1)S(1)} %bitcast.23, bf16[3,288,128]{2,1,0:T(8,128)(2,1)S(1)} %bitcast.24, ...), custom_call_target="tpu_custom_call" | custom-call | tf_op jit(solution)/shard_map/attend_odd/pallas_call | solution.py:207
  71.5 2.5 %collective-permute-start.8 = (bf16[4,288,128]{2,1,0:T(8,128)(2,1)S(1)}, bf16[4,288,128]{2,1,0:T(8,128)(2,1)S(1)}, u32[]{:S(2)}, u32[]{:S(2)}) collective-permute-start(bf16[4,288,128]{2,1,0:T(8,128)(2,1)S(1)} %get-tuple-element.42), channel_id=1, source_target_pairs={{18,34},{19,35},{34,18},{35,19},{20,36},{21,37},{36,20},{37,21},{2... | collective-permute-start | bytes 884744 | tf_op jit(solution)/shard_map/ppermute | solution.py:257
  74.1 14.4 %all-to-all-start.1 = ((bf16[8,12,24,128]{3,2,1,0:T(8,128)(2,1)}), bf16[8,12,24,128]{3,2,1,0:T(8,128)(2,1)S(1)}, u32[]{:S(2)}, u32[]{:S(2)}) async-start(bf16[8,12,24,128]{3,2,1,0:T(8,128)(2,1)} %bitcast.5), calls=%async_computation.1 | async-start | bytes 1179648 | tf_op jit(solution)/shard_map/all_to_all | solution.py:67
  88.5 0.0 collective-permute-done.8
  88.6 6.1 %collective-permute-start.9 = (bf16[2,12,24,128]{3,2,1,0:T(8,128)(2,1)S(1)}, bf16[2,12,24,128]{3,2,1,0:T(8,128)(2,1)S(1)}, u32[]{:S(2)}, u32[]{:S(2)}) collective-permute-start(bf16[2,12,24,128]{3,2,1,0:T(8,128)(2,1)S(1)} %bitcast.29), channel_id=1, source_target_pairs={{20,18},{21,19},{36,34},{37,35},{18,20},{19,21},{34,36},{35,37},{2... | collective-permute-start | bytes 442376 | tf_op jit(solution)/shard_map/ppermute | solution.py:261
  94.8 2.6 %collective-permute-start.10 = (bf16[2,12,24,128]{3,2,1,0:T(8,128)(2,1)S(1)}, bf16[2,12,24,128]{3,2,1,0:T(8,128)(2,1)S(1)}, u32[]{:S(2)}, u32[]{:S(2)}) collective-permute-start(bf16[2,12,24,128]{3,2,1,0:T(8,128)(2,1)S(1)} %bitcast.30), channel_id=1, source_target_pairs={{19,18},{18,19},{35,34},{34,35},{21,20},{20,21},{37,36},{36,37},{2... | collective-permute-start | bytes 442376 | tf_op jit(solution)/shard_map/ppermute | solution.py:261
  97.4 6.6 %collective-permute-start.11 = (bf16[2,12,24,128]{3,2,1,0:T(8,128)(2,1)S(1)}, bf16[2,12,24,128]{3,2,1,0:T(8,128)(2,1)S(1)}, u32[]{:S(2)}, u32[]{:S(2)}) collective-permute-start(bf16[2,12,24,128]{3,2,1,0:T(8,128)(2,1)S(1)} %bitcast.31), channel_id=1, source_target_pairs={{21,18},{20,19},{37,34},{36,35},{19,20},{18,21},{35,36},{34,37},{2... | collective-permute-start | bytes 442376 | tf_op jit(solution)/shard_map/ppermute | solution.py:261
  104.1 3.4 %collective-permute-start.12 = (bf16[2,12,24,128]{3,2,1,0:T(8,128)(2,1)S(1)}, bf16[2,12,24,128]{3,2,1,0:T(8,128)(2,1)S(1)}, u32[]{:S(2)}, u32[]{:S(2)}) collective-permute-start(bf16[2,12,24,128]{3,2,1,0:T(8,128)(2,1)S(1)} %bitcast.32), channel_id=1, source_target_pairs={{18,18},{19,19},{34,34},{35,35},{20,20},{21,21},{36,36},{37,37},{2... | collective-permute-start | bytes 442376 | tf_op jit(solution)/shard_map/ppermute | solution.py:261
  107.4 0.0 collective-permute-done.9.refs_0_
  107.5 0.0 copy-start.5
  107.5 0.0 collective-permute-done.10.refs_1_
  107.5 0.0 copy-start.6
  107.5 0.0 collective-permute-done.11.refs_2_
  107.5 0.0 copy-start.7
  107.5 4.5 %collective-permute-done.12.refs_3_ = bf16[2,12,24,128]{3,2,1,0:T(8,128)(2,1)S(1)} collective-permute-done((bf16[2,12,24,128]{3,2,1,0:T(8,128)(2,1)S(1)}, bf16[2,12,24,128]{3,2,1,0:T(8,128)(2,1)S(1)}, u32[]{:S(2)}, u32[]{:S(2)}) %collective-permute-start.12) | collective-permute-done | bytes 147488 | tf_op jit(solution)/shard_map/ppermute | solution.py:261
  112.1 0.0 all-to-all-done.1.even_ref
  112.1 0.0 copy-done.5
  112.1 0.0 copy-done.6
  112.1 0.6 copy-done.8
  112.7 0.8 copy-done.4
  113.5 3.2 %join_heads.1 = bf16[12,48,1024]{2,1,0:T(8,128)(2,1)} custom-call(s32[2]{0:T(128)} %copy-done.3, bf16[8,12,24,128]{3,2,1,0:T(8,128)(2,1)} %copy-done.4, bf16[2,12,24,128]{3,2,1,0:T(8,128)(2,1)} %copy-done.5, bf16[2,12,24,128]{3,2,1,0:T(8,128)(2,1)} %copy-done.6, bf16[2,12,24,128]{3,2,1,0:T(8,128)(2,1)} %copy-done.7, bf16[2,12,24,128]{3,2,1,0:T(8,128)(2,1)} %copy-done.8), custom_call_target="tpu_custom_call" | custom-call | tf_op jit(solution)/shard_map/join_heads/pallas_call | solution.py:136
  (12 shorter events, 0.1 us)
Async XLA Ops:
  0.1 11.3 %copy-start.3 = (s32[2]{0:T(128)}, s32[2]{0:T(128)S(1)}, u32[]{:S(2)}) copy-start(s32[2]{0:T(128)S(1)} %pad_add_fusion.where_ref) | copy-start | bytes 28
  0.1 2.0 %copy-start = (bf16[3,1,12,48,1024]{4,3,2,1,0:T(8,128)(2,1)S(1)}, bf16[3,1,12,48,1024]{4,3,2,1,0:T(8,128)(2,1)}, u32[]{:S(2)}) copy-start(bf16[3,1,12,48,1024]{4,3,2,1,0:T(8,128)(2,1)} %param.1) | copy-start | bytes 10616836
  3.1 1.2 %copy-start.2 = (bf16[8,3,12,24,128]{4,3,2,1,0:T(8,128)(2,1)}, bf16[8,3,12,24,128]{4,3,2,1,0:T(8,128)(2,1)S(1)}, u32[]{:S(2)}) copy-start(bf16[8,3,12,24,128]{4,3,2,1,0:T(8,128)(2,1)S(1)} %split_even.1) | copy-start | bytes 5308420
  4.3 7.1 %copy-start.1 = (bf16[3,1,12,48,1024]{4,3,2,1,0:T(8,128)(2,1)S(1)}, bf16[3,1,12,48,1024]{4,3,2,1,0:T(8,128)(2,1)}, u32[]{:S(2)}) copy-start(bf16[3,1,12,48,1024]{4,3,2,1,0:T(8,128)(2,1)} %param.1) | copy-start | bytes 10616836
  4.3 49.6 %all-to-all-start = ((bf16[8,3,12,24,128]{4,3,2,1,0:T(8,128)(2,1)}), bf16[8,3,12,24,128]{4,3,2,1,0:T(8,128)(2,1)}, u32[]{:S(2)}, u32[]{:S(2)}) async-start(bf16[8,3,12,24,128]{4,3,2,1,0:T(8,128)(2,1)} %copy-done.2), calls=%async_computation | async-start | bytes 3538944 | tf_op jit(solution)/shard_map/all_to_all | solution.py:67
  13.2 29.6 %collective-permute-start = (bf16[3,12,24,128]{3,2,1,0:T(8,128)(2,1)S(1)}, bf16[3,12,24,128]{3,2,1,0:T(8,128)(2,1)S(1)}, u32[]{:S(2)}, u32[]{:S(2)}) collective-permute-start(bf16[3,12,24,128]{3,2,1,0:T(8,128)(2,1)S(1)} %get-tuple-element.24), channel_id=1, source_target_pairs={{18,34},{19,35},{34,18},{35,19},{20,36},{21,37},{36,20},{37,21},{2... | collective-permute-start | bytes 663560 | tf_op jit(solution)/shard_map/ppermute | solution.py:238
  27.1 17.7 %collective-permute-start.1 = (bf16[3,12,24,128]{3,2,1,0:T(8,128)(2,1)S(1)}, bf16[3,12,24,128]{3,2,1,0:T(8,128)(2,1)S(1)}, u32[]{:S(2)}, u32[]{:S(2)}) collective-permute-start(bf16[3,12,24,128]{3,2,1,0:T(8,128)(2,1)S(1)} %get-tuple-element.25), channel_id=1, source_target_pairs={{18,19},{19,18},{34,35},{35,34},{20,21},{21,20},{36,37},{37,36},{2... | collective-permute-start | bytes 663560 | tf_op jit(solution)/shard_map/ppermute | solution.py:238
  29.1 18.9 %collective-permute-start.2 = (bf16[3,12,24,128]{3,2,1,0:T(8,128)(2,1)S(1)}, bf16[3,12,24,128]{3,2,1,0:T(8,128)(2,1)S(1)}, u32[]{:S(2)}, u32[]{:S(2)}) collective-permute-start(bf16[3,12,24,128]{3,2,1,0:T(8,128)(2,1)S(1)} %get-tuple-element.26), channel_id=1, source_target_pairs={{18,20},{19,21},{34,36},{35,37},{20,18},{21,19},{36,34},{37,35},{2... | collective-permute-start | bytes 663560 | tf_op jit(solution)/shard_map/ppermute | solution.py:238
  32.3 31.4 %collective-permute-start.3 = (bf16[3,12,24,128]{3,2,1,0:T(8,128)(2,1)}, bf16[3,12,24,128]{3,2,1,0:T(8,128)(2,1)S(1)}, u32[]{:S(2)}, u32[]{:S(2)}) collective-permute-start(bf16[3,12,24,128]{3,2,1,0:T(8,128)(2,1)} %get-tuple-element.27), channel_id=1, source_target_pairs={{18,35},{19,34},{34,19},{35,18},{20,37},{21,36},{36,21},{37,20},{2... | collective-permute-start | bytes 663560 | tf_op jit(solution)/shard_map/ppermute | solution.py:238
  34.3 29.5 %collective-permute-start.4 = (bf16[3,12,24,128]{3,2,1,0:T(8,128)(2,1)}, bf16[3,12,24,128]{3,2,1,0:T(8,128)(2,1)S(1)}, u32[]{:S(2)}, u32[]{:S(2)}) collective-permute-start(bf16[3,12,24,128]{3,2,1,0:T(8,128)(2,1)} %get-tuple-element.28), channel_id=1, source_target_pairs={{18,36},{19,37},{34,20},{35,21},{20,34},{21,35},{36,18},{37,19},{2... | collective-permute-start | bytes 663560 | tf_op jit(solution)/shard_map/ppermute | solution.py:238
  42.9 20.9 %collective-permute-start.5 = (bf16[3,12,24,128]{3,2,1,0:T(8,128)(2,1)}, bf16[3,12,24,128]{3,2,1,0:T(8,128)(2,1)S(1)}, u32[]{:S(2)}, u32[]{:S(2)}) collective-permute-start(bf16[3,12,24,128]{3,2,1,0:T(8,128)(2,1)} %get-tuple-element.29), channel_id=1, source_target_pairs={{18,21},{19,20},{34,37},{35,36},{20,19},{21,18},{36,35},{37,34},{2... | collective-permute-start | bytes 663560 | tf_op jit(solution)/shard_map/ppermute | solution.py:238
  44.8 19.0 %collective-permute-start.6 = (bf16[3,12,24,128]{3,2,1,0:T(8,128)(2,1)}, bf16[3,12,24,128]{3,2,1,0:T(8,128)(2,1)S(1)}, u32[]{:S(2)}, u32[]{:S(2)}) collective-permute-start(bf16[3,12,24,128]{3,2,1,0:T(8,128)(2,1)} %get-tuple-element.30), channel_id=1, source_target_pairs={{18,37},{19,36},{34,21},{35,20},{20,35},{21,34},{36,19},{37,18},{2... | collective-permute-start | bytes 663560 | tf_op jit(solution)/shard_map/ppermute | solution.py:238
  47.9 15.9 %collective-permute-start.7 = (bf16[3,12,24,128]{3,2,1,0:T(8,128)(2,1)}, bf16[3,12,24,128]{3,2,1,0:T(8,128)(2,1)S(1)}, u32[]{:S(2)}, u32[]{:S(2)}) collective-permute-start(bf16[3,12,24,128]{3,2,1,0:T(8,128)(2,1)} %get-tuple-element.31), channel_id=1, source_target_pairs={{18,18},{19,19},{34,34},{35,35},{20,20},{21,21},{36,36},{37,37},{2... | collective-permute-start | bytes 663560 | tf_op jit(solution)/shard_map/ppermute | solution.py:238
  71.5 17.0 %collective-permute-start.8 = (bf16[4,288,128]{2,1,0:T(8,128)(2,1)S(1)}, bf16[4,288,128]{2,1,0:T(8,128)(2,1)S(1)}, u32[]{:S(2)}, u32[]{:S(2)}) collective-permute-start(bf16[4,288,128]{2,1,0:T(8,128)(2,1)S(1)} %get-tuple-element.42), channel_id=1, source_target_pairs={{18,34},{19,35},{34,18},{35,19},{20,36},{21,37},{36,20},{37,21},{2... | collective-permute-start | bytes 884744 | tf_op jit(solution)/shard_map/ppermute | solution.py:257
  74.1 38.0 %all-to-all-start.1 = ((bf16[8,12,24,128]{3,2,1,0:T(8,128)(2,1)}), bf16[8,12,24,128]{3,2,1,0:T(8,128)(2,1)S(1)}, u32[]{:S(2)}, u32[]{:S(2)}) async-start(bf16[8,12,24,128]{3,2,1,0:T(8,128)(2,1)} %bitcast.5), calls=%async_computation.1 | async-start | bytes 1179648 | tf_op jit(solution)/shard_map/all_to_all | solution.py:67
  88.6 18.9 %collective-permute-start.9 = (bf16[2,12,24,128]{3,2,1,0:T(8,128)(2,1)S(1)}, bf16[2,12,24,128]{3,2,1,0:T(8,128)(2,1)S(1)}, u32[]{:S(2)}, u32[]{:S(2)}) collective-permute-start(bf16[2,12,24,128]{3,2,1,0:T(8,128)(2,1)S(1)} %bitcast.29), channel_id=1, source_target_pairs={{20,18},{21,19},{36,34},{37,35},{18,20},{19,21},{34,36},{35,37},{2... | collective-permute-start | bytes 442376 | tf_op jit(solution)/shard_map/ppermute | solution.py:261
  94.8 12.7 %collective-permute-start.10 = (bf16[2,12,24,128]{3,2,1,0:T(8,128)(2,1)S(1)}, bf16[2,12,24,128]{3,2,1,0:T(8,128)(2,1)S(1)}, u32[]{:S(2)}, u32[]{:S(2)}) collective-permute-start(bf16[2,12,24,128]{3,2,1,0:T(8,128)(2,1)S(1)} %bitcast.30), channel_id=1, source_target_pairs={{19,18},{18,19},{35,34},{34,35},{21,20},{20,21},{37,36},{36,37},{2... | collective-permute-start | bytes 442376 | tf_op jit(solution)/shard_map/ppermute | solution.py:261
  97.4 10.1 %collective-permute-start.11 = (bf16[2,12,24,128]{3,2,1,0:T(8,128)(2,1)S(1)}, bf16[2,12,24,128]{3,2,1,0:T(8,128)(2,1)S(1)}, u32[]{:S(2)}, u32[]{:S(2)}) collective-permute-start(bf16[2,12,24,128]{3,2,1,0:T(8,128)(2,1)S(1)} %bitcast.31), channel_id=1, source_target_pairs={{21,18},{20,19},{37,34},{36,35},{19,20},{18,21},{35,36},{34,37},{2... | collective-permute-start | bytes 442376 | tf_op jit(solution)/shard_map/ppermute | solution.py:261
  104.1 8.0 %collective-permute-start.12 = (bf16[2,12,24,128]{3,2,1,0:T(8,128)(2,1)S(1)}, bf16[2,12,24,128]{3,2,1,0:T(8,128)(2,1)S(1)}, u32[]{:S(2)}, u32[]{:S(2)}) collective-permute-start(bf16[2,12,24,128]{3,2,1,0:T(8,128)(2,1)S(1)} %bitcast.32), channel_id=1, source_target_pairs={{18,18},{19,19},{34,34},{35,35},{20,20},{21,21},{36,36},{37,37},{2... | collective-permute-start | bytes 442376 | tf_op jit(solution)/shard_map/ppermute | solution.py:261
  107.5 4.6 %copy-start.5 = (bf16[2,12,24,128]{3,2,1,0:T(8,128)(2,1)}, bf16[2,12,24,128]{3,2,1,0:T(8,128)(2,1)S(1)}, u32[]{:S(2)}) copy-start(bf16[2,12,24,128]{3,2,1,0:T(8,128)(2,1)S(1)} %collective-permute-done.9.refs_0_) | copy-start | bytes 442372
  107.5 4.6 %copy-start.6 = (bf16[2,12,24,128]{3,2,1,0:T(8,128)(2,1)}, bf16[2,12,24,128]{3,2,1,0:T(8,128)(2,1)S(1)}, u32[]{:S(2)}) copy-start(bf16[2,12,24,128]{3,2,1,0:T(8,128)(2,1)S(1)} %collective-permute-done.10.refs_1_) | copy-start | bytes 442372
  107.5 4.6 %copy-start.7 = (bf16[2,12,24,128]{3,2,1,0:T(8,128)(2,1)}, bf16[2,12,24,128]{3,2,1,0:T(8,128)(2,1)S(1)}, u32[]{:S(2)}) copy-start(bf16[2,12,24,128]{3,2,1,0:T(8,128)(2,1)S(1)} %collective-permute-done.11.refs_2_) | copy-start | bytes 442372
  112.1 0.6 copy-start.8
  112.7 0.8 copy-start.4

commit v5 on v4

--- a/solution.py
+++ b/solution.py
@@ -11,7 +11,7 @@
 HEAD_DIM = 128
 PEERS = 8
 ORDER = (2, 1, 4, 3, 6, 5, 7, 0)
-SIDE = (4, 1, 5, 0)
+SIDE = (5, 1, 4, 0)
 
 
 def flat(band, core, x, z_lo):

time: 117 us -> 117 us (level)
  transfers between devices with their start and end apart: 15 -> 15, of which waited for: 1 -> 2; matrix products, arithmetic and copies ran while one was open for 0% -> 0% of each run, Pallas kernels for 10% -> 10%
where the time goes in v5:
time: 117 us
  starting transfers between devices  83.4 us (71%)
  Pallas kernels  23.6 us (20%)
  local copies, waits for them, and re-layouts  4.69 us (4%)
  waiting for transfers between devices  4.6 us (4%)
    ppermute x8, starting transfers between devices, body(): odd = [lax.ppermute(odd[k], AXES, to_workers(1, k)) for k in ORDER]  40.6 us
    all_to_all x2, starting transfers between devices, exchange(): lax.all_to_all(blocks, AXES, split_axis=0, concat_axis=0, axis_index_grou...  21.5 us
    ppermute x4, starting transfers between devices, body(): odd.append(lax.ppermute(pair, AXES, to_holders(1, d)))  18.8 us
    pallas_call x2, Pallas kernels, attend(): pl.pallas_call(kernel, out_shape=out_shape, in_specs=[pl.BlockSpec(memory...  17.5 us
    unnamed x18, local copies, waits for them, and re-layouts  4.65 us
    ppermute x4, waiting for transfers between devices, body(): odd.append(lax.ppermute(pair, AXES, to_holders(1, d)))  4.57 us
    pallas_call x1, Pallas kernels, join_heads(): pl.pallas_call(join_kernel, out_shape=jax.ShapeDtypeStruct((rows, 2 * hal...  3.16 us
    pallas_call x2, Pallas kernels, cut(): pl.pallas_call(kernel, out_shape=out_shape, grid_spec=pltpu.PrefetchScala...  2.88 us
  transfers between devices with their start and end apart: 15, of which 2 were waited for; matrix products, arithmetic and copies ran while one was open for 0% of the time, Pallas kernels for 10%

profile of v5, /device:TPU:65, one launch (start us, length us, event | category | flops | bytes accessed | tf_op | source)
XLA Modules:
  0.0 116.7 jit_solution(11966693757868281933)
XLA Ops:
  0.0 0.1 pad_add_fusion.where_ref
  0.1 2.0 %copy-done = bf16[3,1,12,48,1024]{4,3,2,1,0:T(8,128)(2,1)S(1)} copy-done((bf16[3,1,12,48,1024]{4,3,2,1,0:T(8,128)(2,1)S(1)}, bf16[3,1,12,48,1024]{4,3,2,1,0:T(8,128)(2,1)}, u32[]{:S(2)}) %copy-start) | copy-done | bytes 3538968
  2.1 1.0 split_even.1
  3.1 0.0 copy-start.2
  3.1 1.2 %copy-done.2 = bf16[8,3,12,24,128]{4,3,2,1,0:T(8,128)(2,1)} copy-done((bf16[8,3,12,24,128]{4,3,2,1,0:T(8,128)(2,1)}, bf16[8,3,12,24,128]{4,3,2,1,0:T(8,128)(2,1)S(1)}, u32[]{:S(2)}) %copy-start.2) | copy-done | bytes 1769496
  4.3 7.1 %all-to-all-start = ((bf16[8,3,12,24,128]{4,3,2,1,0:T(8,128)(2,1)}), bf16[8,3,12,24,128]{4,3,2,1,0:T(8,128)(2,1)}, u32[]{:S(2)}, u32[]{:S(2)}) async-start(bf16[8,3,12,24,128]{4,3,2,1,0:T(8,128)(2,1)} %copy-done.2), calls=%async_computation | async-start | bytes 3538944 | tf_op jit(solution)/shard_map/all_to_all | solution.py:67
  11.3 0.0 copy-done.3
  11.3 0.0 copy-done.1
  11.3 1.9 %split_odd.1 = (bf16[3,12,24,128]{3,2,1,0:T(8,128)(2,1)}, bf16[3,12,24,128]{3,2,1,0:T(8,128)(2,1)S(1)}, bf16[3,12,24,128]{3,2,1,0:T(8,128)(2,1)S(1)}, bf16[3,12,...) custom-call(s32[2]{0:T(128)S(1)} %pad_add_fusion.where_ref, ...), custom_call_target="tpu_custom_call" | custom-call | tf_op jit(solution)/shard_map/split_odd/pallas_call | solution.py:95
  13.2 13.9 %collective-permute-start = (bf16[3,12,24,128]{3,2,1,0:T(8,128)(2,1)S(1)}, bf16[3,12,24,128]{3,2,1,0:T(8,128)(2,1)S(1)}, u32[]{:S(2)}, u32[]{:S(2)}) collective-permute-start(bf16[3,12,24,128]{3,2,1,0:T(8,128)(2,1)S(1)} %get-tuple-element.24), channel_id=1, source_target_pairs={{18,34},{19,35},{34,18},{35,19},{20,36},{21,37},{36,20},{37,21},{2... | collective-permute-start | bytes 663560 | tf_op jit(solution)/shard_map/ppermute | solution.py:238
  27.1 1.9 %collective-permute-start.1 = (bf16[3,12,24,128]{3,2,1,0:T(8,128)(2,1)S(1)}, bf16[3,12,24,128]{3,2,1,0:T(8,128)(2,1)S(1)}, u32[]{:S(2)}, u32[]{:S(2)}) collective-permute-start(bf16[3,12,24,128]{3,2,1,0:T(8,128)(2,1)S(1)} %get-tuple-element.25), channel_id=1, source_target_pairs={{18,19},{19,18},{34,35},{35,34},{20,21},{21,20},{36,37},{37,36},{2... | collective-permute-start | bytes 663560 | tf_op jit(solution)/shard_map/ppermute | solution.py:238
  29.1 3.3 %collective-permute-start.2 = (bf16[3,12,24,128]{3,2,1,0:T(8,128)(2,1)S(1)}, bf16[3,12,24,128]{3,2,1,0:T(8,128)(2,1)S(1)}, u32[]{:S(2)}, u32[]{:S(2)}) collective-permute-start(bf16[3,12,24,128]{3,2,1,0:T(8,128)(2,1)S(1)} %get-tuple-element.26), channel_id=1, source_target_pairs={{18,20},{19,21},{34,36},{35,37},{20,18},{21,19},{36,34},{37,35},{2... | collective-permute-start | bytes 663560 | tf_op jit(solution)/shard_map/ppermute | solution.py:238
  32.3 1.9 %collective-permute-start.3 = (bf16[3,12,24,128]{3,2,1,0:T(8,128)(2,1)}, bf16[3,12,24,128]{3,2,1,0:T(8,128)(2,1)S(1)}, u32[]{:S(2)}, u32[]{:S(2)}) collective-permute-start(bf16[3,12,24,128]{3,2,1,0:T(8,128)(2,1)} %get-tuple-element.27), channel_id=1, source_target_pairs={{18,35},{19,34},{34,19},{35,18},{20,37},{21,36},{36,21},{37,20},{2... | collective-permute-start | bytes 663560 | tf_op jit(solution)/shard_map/ppermute | solution.py:238
  34.3 8.6 %collective-permute-start.4 = (bf16[3,12,24,128]{3,2,1,0:T(8,128)(2,1)}, bf16[3,12,24,128]{3,2,1,0:T(8,128)(2,1)S(1)}, u32[]{:S(2)}, u32[]{:S(2)}) collective-permute-start(bf16[3,12,24,128]{3,2,1,0:T(8,128)(2,1)} %get-tuple-element.28), channel_id=1, source_target_pairs={{18,36},{19,37},{34,20},{35,21},{20,34},{21,35},{36,18},{37,19},{2... | collective-permute-start | bytes 663560 | tf_op jit(solution)/shard_map/ppermute | solution.py:238
  42.9 0.0 collective-permute-done
  42.9 1.9 %collective-permute-start.5 = (bf16[3,12,24,128]{3,2,1,0:T(8,128)(2,1)}, bf16[3,12,24,128]{3,2,1,0:T(8,128)(2,1)S(1)}, u32[]{:S(2)}, u32[]{:S(2)}) collective-permute-start(bf16[3,12,24,128]{3,2,1,0:T(8,128)(2,1)} %get-tuple-element.29), channel_id=1, source_target_pairs={{18,21},{19,20},{34,37},{35,36},{20,19},{21,18},{36,35},{37,34},{2... | collective-permute-start | bytes 663560 | tf_op jit(solution)/shard_map/ppermute | solution.py:238
  44.8 0.0 collective-permute-done.1
  44.8 3.1 %collective-permute-start.6 = (bf16[3,12,24,128]{3,2,1,0:T(8,128)(2,1)}, bf16[3,12,24,128]{3,2,1,0:T(8,128)(2,1)S(1)}, u32[]{:S(2)}, u32[]{:S(2)}) collective-permute-start(bf16[3,12,24,128]{3,2,1,0:T(8,128)(2,1)} %get-tuple-element.30), channel_id=1, source_target_pairs={{18,37},{19,36},{34,21},{35,20},{20,35},{21,34},{36,19},{37,18},{2... | collective-permute-start | bytes 663560 | tf_op jit(solution)/shard_map/ppermute | solution.py:238
  47.9 0.0 collective-permute-done.2
  47.9 6.0 %collective-permute-start.7 = (bf16[3,12,24,128]{3,2,1,0:T(8,128)(2,1)}, bf16[3,12,24,128]{3,2,1,0:T(8,128)(2,1)S(1)}, u32[]{:S(2)}, u32[]{:S(2)}) collective-permute-start(bf16[3,12,24,128]{3,2,1,0:T(8,128)(2,1)} %get-tuple-element.31), channel_id=1, source_target_pairs={{18,18},{19,19},{34,34},{35,35},{20,20},{21,21},{36,36},{37,37},{2... | collective-permute-start | bytes 663560 | tf_op jit(solution)/shard_map/ppermute | solution.py:238
  53.9 0.0 all-to-all-done
  53.9 9.9 %attend_even.1 = bf16[8,288,128]{2,1,0:T(8,128)(2,1)} custom-call(s32[1]{0:T(128)} %bitcast.2.split_ref, bf16[8,3,288,128]{3,2,1,0:T(8,128)(2,1)} %bitcast.4.qkv_ref), custom_call_target="tpu_custom_call" | custom-call | tf_op jit(solution)/shard_map/attend_even/pallas_call | solution.py:207
  63.8 0.0 collective-permute-done.3
  63.8 0.0 collective-permute-done.4
  63.8 0.0 collective-permute-done.5
  63.8 0.0 collective-permute-done.6
  63.8 0.0 collective-permute-done.7
  63.8 7.7 %attend_odd.1 = (bf16[4,288,128]{2,1,0:T(8,128)(2,1)S(1)}, bf16[4,288,128]{2,1,0:T(8,128)(2,1)S(1)}) custom-call(s32[1]{0:T(128)} %bitcast.2.split_ref, bf16[3,288,128]{2,1,0:T(8,128)(2,1)S(1)} %bitcast.21, bf16[3,288,128]{2,1,0:T(8,128)(2,1)S(1)} %bitcast.22, bf16[3,288,128]{2,1,0:T(8,128)(2,1)S(1)} %bitcast.23, bf16[3,288,128]{2,1,0:T(8,128)(2,1)S(1)} %bitcast.24, ...), custom_call_target="tpu_custom_call" | custom-call | tf_op jit(solution)/shard_map/attend_odd/pallas_call | solution.py:207
  71.5 2.5 %collective-permute-start.8 = (bf16[4,288,128]{2,1,0:T(8,128)(2,1)S(1)}, bf16[4,288,128]{2,1,0:T(8,128)(2,1)S(1)}, u32[]{:S(2)}, u32[]{:S(2)}) collective-permute-start(bf16[4,288,128]{2,1,0:T(8,128)(2,1)S(1)} %get-tuple-element.42), channel_id=1, source_target_pairs={{18,34},{19,35},{34,18},{35,19},{20,36},{21,37},{36,20},{37,21},{2... | collective-permute-start | bytes 884744 | tf_op jit(solution)/shard_map/ppermute | solution.py:257
  74.1 14.4 %all-to-all-start.1 = ((bf16[8,12,24,128]{3,2,1,0:T(8,128)(2,1)}), bf16[8,12,24,128]{3,2,1,0:T(8,128)(2,1)S(1)}, u32[]{:S(2)}, u32[]{:S(2)}) async-start(bf16[8,12,24,128]{3,2,1,0:T(8,128)(2,1)} %bitcast.5), calls=%async_computation.1 | async-start | bytes 1179648 | tf_op jit(solution)/shard_map/all_to_all | solution.py:67
  88.5 0.0 collective-permute-done.8
  88.6 6.6 %collective-permute-start.9 = (bf16[2,12,24,128]{3,2,1,0:T(8,128)(2,1)S(1)}, bf16[2,12,24,128]{3,2,1,0:T(8,128)(2,1)S(1)}, u32[]{:S(2)}, u32[]{:S(2)}) collective-permute-start(bf16[2,12,24,128]{3,2,1,0:T(8,128)(2,1)S(1)} %bitcast.29), channel_id=1, source_target_pairs={{21,18},{20,19},{37,34},{36,35},{19,20},{18,21},{35,36},{34,37},{2... | collective-permute-start | bytes 442376 | tf_op jit(solution)/shard_map/ppermute | solution.py:261
  95.2 1.9 %collective-permute-start.10 = (bf16[2,12,24,128]{3,2,1,0:T(8,128)(2,1)S(1)}, bf16[2,12,24,128]{3,2,1,0:T(8,128)(2,1)S(1)}, u32[]{:S(2)}, u32[]{:S(2)}) collective-permute-start(bf16[2,12,24,128]{3,2,1,0:T(8,128)(2,1)S(1)} %bitcast.30), channel_id=1, source_target_pairs={{19,18},{18,19},{35,34},{34,35},{21,20},{20,21},{37,36},{36,37},{2... | collective-permute-start | bytes 442376 | tf_op jit(solution)/shard_map/ppermute | solution.py:261
  97.1 6.9 %collective-permute-start.11 = (bf16[2,12,24,128]{3,2,1,0:T(8,128)(2,1)S(1)}, bf16[2,12,24,128]{3,2,1,0:T(8,128)(2,1)S(1)}, u32[]{:S(2)}, u32[]{:S(2)}) collective-permute-start(bf16[2,12,24,128]{3,2,1,0:T(8,128)(2,1)S(1)} %bitcast.31), channel_id=1, source_target_pairs={{20,18},{21,19},{36,34},{37,35},{18,20},{19,21},{34,36},{35,37},{2... | collective-permute-start | bytes 442376 | tf_op jit(solution)/shard_map/ppermute | solution.py:261
  104.1 3.4 %collective-permute-start.12 = (bf16[2,12,24,128]{3,2,1,0:T(8,128)(2,1)S(1)}, bf16[2,12,24,128]{3,2,1,0:T(8,128)(2,1)S(1)}, u32[]{:S(2)}, u32[]{:S(2)}) collective-permute-start(bf16[2,12,24,128]{3,2,1,0:T(8,128)(2,1)S(1)} %bitcast.32), channel_id=1, source_target_pairs={{18,18},{19,19},{34,34},{35,35},{20,20},{21,21},{36,36},{37,37},{2... | collective-permute-start | bytes 442376 | tf_op jit(solution)/shard_map/ppermute | solution.py:261
  107.4 0.0 collective-permute-done.9.refs_0_
  107.5 0.0 copy-start.5
  107.5 0.0 collective-permute-done.10.refs_1_
  107.5 0.0 copy-start.6
  107.5 0.3 collective-permute-done.11.refs_2_
  107.8 4.2 %collective-permute-done.12.refs_3_ = bf16[2,12,24,128]{3,2,1,0:T(8,128)(2,1)S(1)} collective-permute-done((bf16[2,12,24,128]{3,2,1,0:T(8,128)(2,1)S(1)}, bf16[2,12,24,128]{3,2,1,0:T(8,128)(2,1)S(1)}, u32[]{:S(2)}, u32[]{:S(2)}) %collective-permute-start.12) | collective-permute-done | bytes 147488 | tf_op jit(solution)/shard_map/ppermute | solution.py:261
  112.1 0.0 all-to-all-done.1.even_ref
  112.1 0.0 copy-done.5
  112.1 0.0 copy-done.6
  112.1 0.0 copy-done.7
  112.1 0.6 copy-done.8
  112.7 0.8 copy-done.4
  113.5 3.2 %join_heads.1 = bf16[12,48,1024]{2,1,0:T(8,128)(2,1)} custom-call(s32[2]{0:T(128)} %copy-done.3, bf16[8,12,24,128]{3,2,1,0:T(8,128)(2,1)} %copy-done.4, bf16[2,12,24,128]{3,2,1,0:T(8,128)(2,1)} %copy-done.5, bf16[2,12,24,128]{3,2,1,0:T(8,128)(2,1)} %copy-done.6, bf16[2,12,24,128]{3,2,1,0:T(8,128)(2,1)} %copy-done.7, bf16[2,12,24,128]{3,2,1,0:T(8,128)(2,1)} %copy-done.8), custom_call_target="tpu_custom_call" | custom-call | tf_op jit(solution)/shard_map/join_heads/pallas_call | solution.py:136
  (12 shorter events, 0.1 us)
Async XLA Ops:
  0.1 11.3 %copy-start.3 = (s32[2]{0:T(128)}, s32[2]{0:T(128)S(1)}, u32[]{:S(2)}) copy-start(s32[2]{0:T(128)S(1)} %pad_add_fusion.where_ref) | copy-start | bytes 28
  0.1 2.0 %copy-start = (bf16[3,1,12,48,1024]{4,3,2,1,0:T(8,128)(2,1)S(1)}, bf16[3,1,12,48,1024]{4,3,2,1,0:T(8,128)(2,1)}, u32[]{:S(2)}) copy-start(bf16[3,1,12,48,1024]{4,3,2,1,0:T(8,128)(2,1)} %param.1) | copy-start | bytes 10616836
  3.1 1.2 %copy-start.2 = (bf16[8,3,12,24,128]{4,3,2,1,0:T(8,128)(2,1)}, bf16[8,3,12,24,128]{4,3,2,1,0:T(8,128)(2,1)S(1)}, u32[]{:S(2)}) copy-start(bf16[8,3,12,24,128]{4,3,2,1,0:T(8,128)(2,1)S(1)} %split_even.1) | copy-start | bytes 5308420
  4.3 7.1 %copy-start.1 = (bf16[3,1,12,48,1024]{4,3,2,1,0:T(8,128)(2,1)S(1)}, bf16[3,1,12,48,1024]{4,3,2,1,0:T(8,128)(2,1)}, u32[]{:S(2)}) copy-start(bf16[3,1,12,48,1024]{4,3,2,1,0:T(8,128)(2,1)} %param.1) | copy-start | bytes 10616836
  4.3 49.6 %all-to-all-start = ((bf16[8,3,12,24,128]{4,3,2,1,0:T(8,128)(2,1)}), bf16[8,3,12,24,128]{4,3,2,1,0:T(8,128)(2,1)}, u32[]{:S(2)}, u32[]{:S(2)}) async-start(bf16[8,3,12,24,128]{4,3,2,1,0:T(8,128)(2,1)} %copy-done.2), calls=%async_computation | async-start | bytes 3538944 | tf_op jit(solution)/shard_map/all_to_all | solution.py:67
  13.2 29.6 %collective-permute-start = (bf16[3,12,24,128]{3,2,1,0:T(8,128)(2,1)S(1)}, bf16[3,12,24,128]{3,2,1,0:T(8,128)(2,1)S(1)}, u32[]{:S(2)}, u32[]{:S(2)}) collective-permute-start(bf16[3,12,24,128]{3,2,1,0:T(8,128)(2,1)S(1)} %get-tuple-element.24), channel_id=1, source_target_pairs={{18,34},{19,35},{34,18},{35,19},{20,36},{21,37},{36,20},{37,21},{2... | collective-permute-start | bytes 663560 | tf_op jit(solution)/shard_map/ppermute | solution.py:238
  27.1 17.7 %collective-permute-start.1 = (bf16[3,12,24,128]{3,2,1,0:T(8,128)(2,1)S(1)}, bf16[3,12,24,128]{3,2,1,0:T(8,128)(2,1)S(1)}, u32[]{:S(2)}, u32[]{:S(2)}) collective-permute-start(bf16[3,12,24,128]{3,2,1,0:T(8,128)(2,1)S(1)} %get-tuple-element.25), channel_id=1, source_target_pairs={{18,19},{19,18},{34,35},{35,34},{20,21},{21,20},{36,37},{37,36},{2... | collective-permute-start | bytes 663560 | tf_op jit(solution)/shard_map/ppermute | solution.py:238
  29.1 18.9 %collective-permute-start.2 = (bf16[3,12,24,128]{3,2,1,0:T(8,128)(2,1)S(1)}, bf16[3,12,24,128]{3,2,1,0:T(8,128)(2,1)S(1)}, u32[]{:S(2)}, u32[]{:S(2)}) collective-permute-start(bf16[3,12,24,128]{3,2,1,0:T(8,128)(2,1)S(1)} %get-tuple-element.26), channel_id=1, source_target_pairs={{18,20},{19,21},{34,36},{35,37},{20,18},{21,19},{36,34},{37,35},{2... | collective-permute-start | bytes 663560 | tf_op jit(solution)/shard_map/ppermute | solution.py:238
  32.3 31.4 %collective-permute-start.3 = (bf16[3,12,24,128]{3,2,1,0:T(8,128)(2,1)}, bf16[3,12,24,128]{3,2,1,0:T(8,128)(2,1)S(1)}, u32[]{:S(2)}, u32[]{:S(2)}) collective-permute-start(bf16[3,12,24,128]{3,2,1,0:T(8,128)(2,1)} %get-tuple-element.27), channel_id=1, source_target_pairs={{18,35},{19,34},{34,19},{35,18},{20,37},{21,36},{36,21},{37,20},{2... | collective-permute-start | bytes 663560 | tf_op jit(solution)/shard_map/ppermute | solution.py:238
  34.3 29.5 %collective-permute-start.4 = (bf16[3,12,24,128]{3,2,1,0:T(8,128)(2,1)}, bf16[3,12,24,128]{3,2,1,0:T(8,128)(2,1)S(1)}, u32[]{:S(2)}, u32[]{:S(2)}) collective-permute-start(bf16[3,12,24,128]{3,2,1,0:T(8,128)(2,1)} %get-tuple-element.28), channel_id=1, source_target_pairs={{18,36},{19,37},{34,20},{35,21},{20,34},{21,35},{36,18},{37,19},{2... | collective-permute-start | bytes 663560 | tf_op jit(solution)/shard_map/ppermute | solution.py:238
  42.9 20.9 %collective-permute-start.5 = (bf16[3,12,24,128]{3,2,1,0:T(8,128)(2,1)}, bf16[3,12,24,128]{3,2,1,0:T(8,128)(2,1)S(1)}, u32[]{:S(2)}, u32[]{:S(2)}) collective-permute-start(bf16[3,12,24,128]{3,2,1,0:T(8,128)(2,1)} %get-tuple-element.29), channel_id=1, source_target_pairs={{18,21},{19,20},{34,37},{35,36},{20,19},{21,18},{36,35},{37,34},{2... | collective-permute-start | bytes 663560 | tf_op jit(solution)/shard_map/ppermute | solution.py:238
  44.8 19.0 %collective-permute-start.6 = (bf16[3,12,24,128]{3,2,1,0:T(8,128)(2,1)}, bf16[3,12,24,128]{3,2,1,0:T(8,128)(2,1)S(1)}, u32[]{:S(2)}, u32[]{:S(2)}) collective-permute-start(bf16[3,12,24,128]{3,2,1,0:T(8,128)(2,1)} %get-tuple-element.30), channel_id=1, source_target_pairs={{18,37},{19,36},{34,21},{35,20},{20,35},{21,34},{36,19},{37,18},{2... | collective-permute-start | bytes 663560 | tf_op jit(solution)/shard_map/ppermute | solution.py:238
  47.9 15.9 %collective-permute-start.7 = (bf16[3,12,24,128]{3,2,1,0:T(8,128)(2,1)}, bf16[3,12,24,128]{3,2,1,0:T(8,128)(2,1)S(1)}, u32[]{:S(2)}, u32[]{:S(2)}) collective-permute-start(bf16[3,12,24,128]{3,2,1,0:T(8,128)(2,1)} %get-tuple-element.31), channel_id=1, source_target_pairs={{18,18},{19,19},{34,34},{35,35},{20,20},{21,21},{36,36},{37,37},{2... | collective-permute-start | bytes 663560 | tf_op jit(solution)/shard_map/ppermute | solution.py:238
  71.5 17.0 %collective-permute-start.8 = (bf16[4,288,128]{2,1,0:T(8,128)(2,1)S(1)}, bf16[4,288,128]{2,1,0:T(8,128)(2,1)S(1)}, u32[]{:S(2)}, u32[]{:S(2)}) collective-permute-start(bf16[4,288,128]{2,1,0:T(8,128)(2,1)S(1)} %get-tuple-element.42), channel_id=1, source_target_pairs={{18,34},{19,35},{34,18},{35,19},{20,36},{21,37},{36,20},{37,21},{2... | collective-permute-start | bytes 884744 | tf_op jit(solution)/shard_map/ppermute | solution.py:257
  74.1 38.0 %all-to-all-start.1 = ((bf16[8,12,24,128]{3,2,1,0:T(8,128)(2,1)}), bf16[8,12,24,128]{3,2,1,0:T(8,128)(2,1)S(1)}, u32[]{:S(2)}, u32[]{:S(2)}) async-start(bf16[8,12,24,128]{3,2,1,0:T(8,128)(2,1)} %bitcast.5), calls=%async_computation.1 | async-start | bytes 1179648 | tf_op jit(solution)/shard_map/all_to_all | solution.py:67
  88.6 18.9 %collective-permute-start.9 = (bf16[2,12,24,128]{3,2,1,0:T(8,128)(2,1)S(1)}, bf16[2,12,24,128]{3,2,1,0:T(8,128)(2,1)S(1)}, u32[]{:S(2)}, u32[]{:S(2)}) collective-permute-start(bf16[2,12,24,128]{3,2,1,0:T(8,128)(2,1)S(1)} %bitcast.29), channel_id=1, source_target_pairs={{21,18},{20,19},{37,34},{36,35},{19,20},{18,21},{35,36},{34,37},{2... | collective-permute-start | bytes 442376 | tf_op jit(solution)/shard_map/ppermute | solution.py:261
  95.2 12.3 %collective-permute-start.10 = (bf16[2,12,24,128]{3,2,1,0:T(8,128)(2,1)S(1)}, bf16[2,12,24,128]{3,2,1,0:T(8,128)(2,1)S(1)}, u32[]{:S(2)}, u32[]{:S(2)}) collective-permute-start(bf16[2,12,24,128]{3,2,1,0:T(8,128)(2,1)S(1)} %bitcast.30), channel_id=1, source_target_pairs={{19,18},{18,19},{35,34},{34,35},{21,20},{20,21},{37,36},{36,37},{2... | collective-permute-start | bytes 442376 | tf_op jit(solution)/shard_map/ppermute | solution.py:261
  97.1 10.7 %collective-permute-start.11 = (bf16[2,12,24,128]{3,2,1,0:T(8,128)(2,1)S(1)}, bf16[2,12,24,128]{3,2,1,0:T(8,128)(2,1)S(1)}, u32[]{:S(2)}, u32[]{:S(2)}) collective-permute-start(bf16[2,12,24,128]{3,2,1,0:T(8,128)(2,1)S(1)} %bitcast.31), channel_id=1, source_target_pairs={{20,18},{21,19},{36,34},{37,35},{18,20},{19,21},{34,36},{35,37},{2... | collective-permute-start | bytes 442376 | tf_op jit(solution)/shard_map/ppermute | solution.py:261
  104.1 8.0 %collective-permute-start.12 = (bf16[2,12,24,128]{3,2,1,0:T(8,128)(2,1)S(1)}, bf16[2,12,24,128]{3,2,1,0:T(8,128)(2,1)S(1)}, u32[]{:S(2)}, u32[]{:S(2)}) collective-permute-start(bf16[2,12,24,128]{3,2,1,0:T(8,128)(2,1)S(1)} %bitcast.32), channel_id=1, source_target_pairs={{18,18},{19,19},{34,34},{35,35},{20,20},{21,21},{36,36},{37,37},{2... | collective-permute-start | bytes 442376 | tf_op jit(solution)/shard_map/ppermute | solution.py:261
  107.5 4.6 %copy-start.5 = (bf16[2,12,24,128]{3,2,1,0:T(8,128)(2,1)}, bf16[2,12,24,128]{3,2,1,0:T(8,128)(2,1)S(1)}, u32[]{:S(2)}) copy-start(bf16[2,12,24,128]{3,2,1,0:T(8,128)(2,1)S(1)} %collective-permute-done.9.refs_0_) | copy-start | bytes 442372
  107.5 4.6 %copy-start.6 = (bf16[2,12,24,128]{3,2,1,0:T(8,128)(2,1)}, bf16[2,12,24,128]{3,2,1,0:T(8,128)(2,1)S(1)}, u32[]{:S(2)}) copy-start(bf16[2,12,24,128]{3,2,1,0:T(8,128)(2,1)S(1)} %collective-permute-done.10.refs_1_) | copy-start | bytes 442372
  107.8 4.3 %copy-start.7 = (bf16[2,12,24,128]{3,2,1,0:T(8,128)(2,1)}, bf16[2,12,24,128]{3,2,1,0:T(8,128)(2,1)S(1)}, u32[]{:S(2)}) copy-start(bf16[2,12,24,128]{3,2,1,0:T(8,128)(2,1)S(1)} %collective-permute-done.11.refs_2_) | copy-start | bytes 442372
  112.1 0.6 copy-start.8
  112.7 0.8 copy-start.4
